TPU v7x, 128 devices: a whole 4x4x4 slice. The times are simulated.
128 devices in a mesh: dp: 32 (over y, x, core), mp: 4 (over z).
Axes of the slice: x: 4, y: 4, z: 4, core: 2. Of those that a mesh axis runs over, the one named last changes fastest.
Arguments:
- query_hidden: bfloat16 [16384, 4096], P('dp'), may hold values from -6 to 6
- passage_hidden: bfloat16 [16384, 4096], P('dp'), may hold values from -6 to 6
- head_weight: bfloat16 [4096, 4096], P(None, 'mp'), may hold values from -0.09375 to 0.09375
- neg_blocks: int32 [128, 4], P('dp'), may hold values from 0 to 127, as said below
- pos_ids: int32 [16384], P('dp'), may hold values from 0 to 127
Outputs:
- query_loss: float32 [16384], P('dp')
- grad_weight: float32 [4096, 4096], P('dp', 'mp')
- grad_query_hidden: bfloat16 [16384, 4096], P('dp', 'mp')
- grad_passage_hidden: bfloat16 [16384, 4096], P('dp', 'mp')
Inputs may be any that keep to these rules, and one draw needn't show every extreme that they name: `neg_blocks`: within each aligned group of 4 query blocks all 16 ids are different, and at most 1 of them fall into any one aligned group of 4 passage block ids; some group of passage blocks receives exactly 1 of them.
All inputs are finite; a program needn't handle non-finite values.
Results may differ from a plain program's by a relative error of at most 0.017.
Values may be sent and summed in bfloat16 or wider, within the bound.
A program may use at most 128 MiB of HBM per device.

v0:
```python
import jax
import jax.numpy as jnp
from jax import lax
from jax.sharding import PartitionSpec as P

logit_divisor = 0.02
epsilon = 1e-06


def back_norm(inverse, unit_rows, d_unit, inner):
    return (inverse[:, None] * (d_unit - unit_rows * inner[:, None])).astype(jnp.bfloat16)


def local(query_hidden, passage_hidden, head_weight, neg_blocks, pos_ids):
    dp_count = lax.axis_size("dp")
    block_count, neg_count = neg_blocks.shape
    row_count = query_hidden.shape[0]
    block_rows = row_count // block_count
    embed_width = head_weight.shape[1]
    cand_rows = (1 + neg_count) * block_rows
    request_count = block_count * neg_count
    slot_depth = (request_count + dp_count - 1) // dp_count
    slot_count = dp_count * slot_depth
    query_embed = jnp.dot(query_hidden, head_weight, preferred_element_type=jnp.float32)
    passage_embed = jnp.dot(passage_hidden, head_weight, preferred_element_type=jnp.float32)
    query_sq, passage_sq = lax.psum(
        (
            jnp.sum(query_embed * query_embed, axis=1),
            jnp.sum(passage_embed * passage_embed, axis=1),
        ),
        "mp",
    )
    query_inv = lax.rsqrt(query_sq + epsilon)
    passage_inv = lax.rsqrt(passage_sq + epsilon)
    query_unit = query_embed * query_inv[:, None]
    passage_unit = passage_embed * passage_inv[:, None]
    query_norm = query_unit.astype(jnp.bfloat16)
    passage_norm = passage_unit.astype(jnp.bfloat16)
    query_blocks = query_norm.reshape(block_count, block_rows, embed_width)
    passage_blocks = passage_norm.reshape(block_count, block_rows, embed_width)
    wanted = neg_blocks.reshape(-1)
    owners = wanted // block_count
    local_ids = wanted % block_count
    request_order = jnp.arange(request_count, dtype=jnp.int32)
    earlier_same = (owners[:, None] == owners[None, :]) & (
        request_order[None, :] < request_order[:, None]
    )
    owner_rank = jnp.sum(earlier_same.astype(jnp.int32), axis=1)
    slot_of = owners * slot_depth + owner_rank
    slot_table = (slot_of[:, None] == jnp.arange(slot_count, dtype=jnp.int32)[None, :]).astype(
        jnp.int32
    )
    requests = jnp.sum(slot_table * (local_ids + 1)[:, None], axis=0).reshape(dp_count, slot_depth)
    asked = lax.all_to_all(requests, "dp", split_axis=0, concat_axis=0, tiled=True).reshape(
        slot_count
    )
    live_slots = (asked > 0).astype(jnp.bfloat16)
    picked = jnp.take(passage_blocks, jnp.maximum(asked - 1, 0), axis=0) * live_slots[:, None, None]
    reply = picked.reshape(dp_count, slot_depth, block_rows, embed_width)
    arrived = lax.all_to_all(reply, "dp", split_axis=0, concat_axis=0, tiled=True).reshape(
        slot_count, block_rows, embed_width
    )
    fetched = jnp.take(arrived, slot_of, axis=0).reshape(
        block_count, neg_count, block_rows, embed_width
    )
    retrieved_documents = jnp.concatenate([passage_blocks[:, None], fetched], axis=1).reshape(
        block_count, cand_rows, embed_width
    )
    similarity_parts = jnp.einsum(
        "bqe,bce->bqc", query_blocks, retrieved_documents, preferred_element_type=jnp.float32
    )
    positions = pos_ids.reshape(block_count, block_rows)
    similarity_table = (
        lax.psum(similarity_parts.astype(jnp.bfloat16), "mp").astype(jnp.float32) / logit_divisor
    )
    columns = jnp.arange(cand_rows, dtype=jnp.int32)
    matching_document_slot = (columns[None, None, :] == positions[:, :, None]).astype(jnp.float32)
    exponent_values = jnp.exp(similarity_table)
    normalizer_totals = jnp.sum(exponent_values, axis=2)
    losses = jnp.log(normalizer_totals) - jnp.sum(similarity_table * matching_document_slot, axis=2)
    attention_probabilities = (
        (exponent_values / normalizer_totals[:, :, None] - matching_document_slot) / logit_divisor
    ).astype(jnp.bfloat16)
    d_query = jnp.einsum(
        "bqc,bce->bqe",
        attention_probabilities,
        retrieved_documents,
        preferred_element_type=jnp.float32,
    ).reshape(row_count, embed_width)
    d_cand = jnp.einsum(
        "bqc,bqe->bce", attention_probabilities, query_blocks, preferred_element_type=jnp.float32
    )
    own_terms = d_cand[:, :block_rows]
    neg_terms = (
        d_cand[:, block_rows:].reshape(request_count, block_rows, embed_width).astype(jnp.bfloat16)
    )
    outgoing = (
        jnp.zeros((slot_count, block_rows, embed_width), jnp.bfloat16).at[slot_of].set(neg_terms)
    )
    outgoing = outgoing.reshape(dp_count, slot_depth, block_rows, embed_width)
    returned = lax.all_to_all(outgoing, "dp", split_axis=0, concat_axis=0, tiled=True).reshape(
        slot_count, block_rows, embed_width
    )
    selector = (asked[None, :] - 1 == jnp.arange(block_count, dtype=jnp.int32)[:, None]).astype(
        jnp.bfloat16
    )
    d_passage = own_terms + jnp.einsum(
        "ls,sbe->lbe", selector, returned, preferred_element_type=jnp.float32
    )
    d_passage = d_passage.reshape(row_count, embed_width)
    query_inner, passage_inner = lax.psum(
        (jnp.sum(query_unit * d_query, axis=1), jnp.sum(passage_unit * d_passage, axis=1)), "mp"
    )
    d_query_embed = back_norm(query_inv, query_unit, d_query, query_inner)
    d_passage_embed = back_norm(passage_inv, passage_unit, d_passage, passage_inner)
    contract = (((0,), (0,)), ((), ()))
    query_part = lax.dot_general(
        query_hidden, d_query_embed, contract, preferred_element_type=jnp.float32
    )
    passage_part = lax.dot_general(
        passage_hidden, d_passage_embed, contract, preferred_element_type=jnp.float32
    )
    grad_weight = lax.psum_scatter(
        (query_part + passage_part).astype(jnp.bfloat16), "dp", scatter_dimension=0, tiled=True
    ).astype(jnp.float32)
    transpose_dims = (((1,), (1,)), ((), ()))
    query_back = lax.dot_general(
        d_query_embed, head_weight, transpose_dims, preferred_element_type=jnp.float32
    ).astype(jnp.bfloat16)
    passage_back = lax.dot_general(
        d_passage_embed, head_weight, transpose_dims, preferred_element_type=jnp.float32
    ).astype(jnp.bfloat16)
    query_grad, passage_grad = (
        lax.psum_scatter(query_back, "mp", scatter_dimension=1, tiled=True).astype(jnp.float32),
        lax.psum_scatter(passage_back, "mp", scatter_dimension=1, tiled=True).astype(jnp.float32),
    )
    return (
        losses.reshape(row_count),
        grad_weight,
        query_grad.astype(jnp.bfloat16),
        passage_grad.astype(jnp.bfloat16),
    )


def solution(mesh):
    placed = (P("dp", None), P("dp", None), P(None, "mp"), P("dp", None), P("dp"))
    return jax.shard_map(
        local,
        mesh=mesh,
        in_specs=placed,
        out_specs=(P("dp"), P("dp", "mp"), P("dp", "mp"), P("dp", "mp")),
        check_vma=False,
    )
```

profile of v0, /device:TPU:1, one launch (start us, length us, event | category | flops | bytes accessed | tf_op | source)
XLA Modules:
  0.0 621.7 jit_solution(7270971885549356364)
XLA Ops:
  7.2 0.8 reshape.267
  8.2 0.7 copy.33
  8.9 8.6 %all-to-all-start = ((s32[32,1,1]{2,1,0:T(1,128)}), s32[32,1,1]{2,1,0:T(1,128)S(1)}, u32[]{:S(2)}, u32[]{:S(2)}) async-start(s32[32,1,1]{2,1,0:T(1,128)} %copy.33), calls=%async_computation | async-start | bytes 32768 | tf_op jit(solution)/shard_map/all_to_all | solution.py:54
  17.5 8.4 %multiply_reduce_fusion.1 = (f32[512]{0:T(512)S(1)}, f32[512,1024]{1,0:T(8,128)S(1)}) fusion(bf16[512,4096]{1,0:T(8,128)(2,1)} %param.5, bf16[4096,1024]{1,0:T(8,128)(2,1)} %param.7), kind=kOutput, calls=%fused_computation.27 | convolution fusion | flops 4296015360 | bytes 14682112 | tf_op jit(solution)/shard_map/dot_general | solution.py:24
  26.0 5.8 multiply_reduce_fusion
  31.8 9.7 %all-reduce.1 = (f32[512]{0:T(512)S(1)}, f32[512]{0:T(512)S(1)}) all-reduce(f32[512]{0:T(512)S(1)} %get-tuple-element.34, f32[512]{0:T(512)S(1)} %get-tuple-element.36), channel_id=1, replica_groups=mesh['dp'=32,'mp'=4] {'mp'}, use_global_device_ids=true, to_apply=%region_3.0 | all-reduce | flops 1024 | bytes 8192 | tf_op jit(solution)/shard_map/psum | solution.py:26
  41.5 1.8 multiply_convert_fusion
  43.3 1.2 add_reduce_fusion
  44.6 4.9 gather_fusion
  49.8 7.4 %fusion.3 = bf16[32,1,128,1024]{3,2,1,0:T(8,128)(2,1)} fusion(bf16[32,128,1024]{2,1,0:T(8,128)(2,1)} %gather_fusion, pred[32]{0:T(512)(128)(4,1)S(1)} %maximum_compare_fusion, bf16[32]{0:T(256)(128)(2,1)S(1)} %fusion.13), kind=kLoop, calls=%fused_computation.9 | loop fusion | flops 8388608 | bytes 16777312 | tf_op jit(solution)/shard_map/mul | solution.py:58
  57.3 9.6 %all-to-all-start.1 = ((bf16[32,1,128,1024]{3,2,1,0:T(8,128)(2,1)}), bf16[32,1,128,1024]{3,2,1,0:T(8,128)(2,1)}, u32[]{:S(2)}, u32[]{:S(2)}) async-start(bf16[32,1,128,1024]{3,2,1,0:T(8,128)(2,1)} %fusion.3), calls=%async_computation.1 | async-start | bytes 16777216 | tf_op jit(solution)/shard_map/all_to_all | solution.py:60
  66.8 0.5 all-reduce.4.cloned.1.call-start
  67.6 1.1 multiply_convert_fusion.1
  68.7 98.8 %all-to-all-done.1 = bf16[32,1,128,1024]{3,2,1,0:T(8,128)(2,1)} async-done(((bf16[32,1,128,1024]{3,2,1,0:T(8,128)(2,1)}), bf16[32,1,128,1024]{3,2,1,0:T(8,128)(2,1)}, u32[]{:S(2)}, u32[]{:S(2)}) %all-to-all-start.1) | async-done | bytes 8388640 | tf_op jit(solution)/shard_map/all_to_all | solution.py:60
  167.5 6.2 gather_fusion.1
  173.7 2.6 broadcast_select_fusion
  176.4 0.5 pad_maximum_fusion
  176.9 2.3 copy-done.1
  179.2 2.6 convolution_convert_fusion.2
  181.8 41.8 %all-reduce.4.cloned.1.call-done = bf16[4,128,640]{2,1,0:T(8,128)(2,1)} async-done(((bf16[4,128,640]{2,1,0:T(8,128)(2,1)}), bf16[4,128,640]{2,1,0:T(8,128)(2,1)}) %all-reduce.4.cloned.1.call-update) | async-done | bytes 655376 | tf_op jit(solution)/shard_map/psum | solution.py:74
  223.7 1.6 fusion.12
  225.2 2.7 fusion.23
  228.0 4.0 copy-done
  232.0 2.7 slice.17
  234.7 4.4 broadcast_in_dim.26
  239.1 11.0 %scatter_fusion = bf16[32,128,1024]{2,1,0:T(8,128)(2,1)} fusion(bf16[32,128,1024]{2,1,0:T(8,128)(2,1)} %broadcast_in_dim.26, s32[16]{0:T(128)S(1)} %fusion.22, bf16[16,128,1024]{2,1,0:T(8,128)(2,1)} %bitcast.76), kind=kCustom, calls=%fused_computation.2 | custom fusion | bytes 12582976 | tf_op jit(solution)/shard_map/scatter | solution.py:98
  250.1 10.1 %all-to-all-start.2 = ((bf16[32,1,128,1024]{3,2,1,0:T(8,128)(2,1)}), bf16[32,1,128,1024]{3,2,1,0:T(8,128)(2,1)}, u32[]{:S(2)}, u32[]{:S(2)}) async-start(bf16[32,1,128,1024]{3,2,1,0:T(8,128)(2,1)} %bitcast.72), calls=%async_computation.2 | async-start | bytes 16777216 | tf_op jit(solution)/shard_map/all_to_all | solution.py:101
  260.4 3.8 fusion.24
  264.3 1.3 copy-done.6
  266.0 94.9 %all-to-all-done.2 = bf16[32,1,128,1024]{3,2,1,0:T(8,128)(2,1)} async-done(((bf16[32,1,128,1024]{3,2,1,0:T(8,128)(2,1)}), bf16[32,1,128,1024]{3,2,1,0:T(8,128)(2,1)}, u32[]{:S(2)}, u32[]{:S(2)}) %all-to-all-start.2) | async-done | bytes 8388640 | tf_op jit(solution)/shard_map/all_to_all | solution.py:101
  360.9 12.4 %fusion.1 = f32[4,128,1024]{2,0,1:T(4,128)S(1)} fusion(bf16[32,1,128,1024]{3,2,1,0:T(8,128)(2,1)} %all-to-all-done.2, s32[32]{0:T(128)S(1)} %get-tuple-element.26), kind=kOutput, calls=%fused_computation.6 | convolution fusion | flops 33554560 | bytes 10485888 | tf_op jit(solution)/shard_map/ls,sbe->lbe/dot_general | solution.py:107
  373.4 3.3 slice_add_fusion
  376.6 1.3 copy-done.3
  378.4 7.2 %all-reduce = (f32[512]{0:T(512)S(1)}, f32[512]{0:T(512)S(1)}) all-reduce(f32[512]{0:T(512)S(1)} %fusion.8, f32[512]{0:T(512)S(1)} %fusion.5), channel_id=1, replica_groups=mesh['dp'=32,'mp'=4] {'mp'}, use_global_device_ids=true, to_apply=%region_10.11 | all-reduce | flops 1024 | bytes 8192 | tf_op jit(solution)/shard_map/psum | solution.py:111
  385.6 2.7 fusion.7
  388.8 1.2 copy-done.8
  390.0 8.1 %fusion.25 = f32[1024,4096]{1,0:T(8,128)} fusion(bf16[512,1024]{1,0:T(8,128)(2,1)S(1)} %fusion.10, bf16[512,4096]{1,0:T(8,128)(2,1)S(1)} %copy-done.8), kind=kOutput, calls=%fused_computation.80 | convolution fusion | flops 4294967296 | bytes 22020096 | tf_op jit(solution)/shard_map/dot_general | solution.py:117
  398.2 11.4 %fusion = bf16[4096,1024]{0,1:T(8,128)(2,1)} fusion(f32[1024,4096]{1,0:T(8,128)} %fusion.25, bf16[512,1024]{1,0:T(8,128)(2,1)S(1)} %fusion.7, bf16[512,4096]{1,0:T(8,128)(2,1)} %param.6), kind=kOutput, calls=%fused_computation.4 | convolution fusion | flops 4303355904 | bytes 30408704 | tf_op jit(solution)/shard_map/dot_general | solution.py:120
  409.5 12.0 %copy.41 = bf16[4096,1024]{1,0:T(8,128)(2,1)} copy(bf16[4096,1024]{0,1:T(8,128)(2,1)} %fusion) | data formatting | bytes 16777216
  421.5 9.5 %convolution_convert_fusion.1 = bf16[512,4096]{1,0:T(8,128)(2,1)} fusion(bf16[512,1024]{1,0:T(8,128)(2,1)S(1)} %fusion.10, bf16[4096,1024]{1,0:T(8,128)(2,1)} %param.7), kind=kOutput, calls=%fused_computation.12 | convolution fusion | flops 4297064448 | bytes 13631488 | tf_op jit(solution)/shard_map/dot_general | solution.py:127
  431.1 1.3 copy-done.11
  432.4 9.9 %convolution_convert_fusion = bf16[512,4096]{1,0:T(8,128)(2,1)} fusion(bf16[512,1024]{1,0:T(8,128)(2,1)S(1)} %copy-done.11, bf16[4096,1024]{1,0:T(8,128)(2,1)} %param.7), kind=kOutput, calls=%fused_computation.11 | convolution fusion | flops 4297064448 | bytes 13631488 | tf_op jit(solution)/shard_map/dot_general | solution.py:130
  442.3 0.6 subtract_bitcast_fusion
  442.9 71.5 %reduce-scatter.10.cloned.1.call-done = bf16[128,1024]{1,0:T(8,128)(2,1)} async-done(((bf16[4096,1024]{1,0:T(8,128)(2,1)}), bf16[128,1024]{1,0:T(8,128)(2,1)}) %reduce-scatter.10.cloned.1.call-update) | async-done | bytes 262160
  514.4 1.1 copy.42
  515.5 0.9 copy.39
  516.4 49.0 %reduce-scatter.6.cloned.1.call-done = bf16[512,1024]{1,0:T(8,128)(2,1)} async-done(((bf16[512,4096]{1,0:T(8,128)(2,1)}), bf16[512,1024]{1,0:T(8,128)(2,1)}) %reduce-scatter.6.cloned.1.call-update) | async-done | bytes 1048592 | tf_op jit(solution)/shard_map/reduce_scatter | solution.py:134
  565.4 49.5 %reduce-scatter.8.cloned.1.call-done = bf16[512,1024]{1,0:T(8,128)(2,1)} async-done(((bf16[512,4096]{1,0:T(8,128)(2,1)}), bf16[512,1024]{1,0:T(8,128)(2,1)}) %reduce-scatter.8.cloned.1.call-update) | async-done | bytes 1048592 | tf_op jit(solution)/shard_map/reduce_scatter | solution.py:135
  (50 shorter events, 2.6 us)
Async XLA Ops:
  8.9 34.4 %all-to-all-start = ((s32[32,1,1]{2,1,0:T(1,128)}), s32[32,1,1]{2,1,0:T(1,128)S(1)}, u32[]{:S(2)}, u32[]{:S(2)}) async-start(s32[32,1,1]{2,1,0:T(1,128)} %copy.33), calls=%async_computation | async-start | bytes 32768 | tf_op jit(solution)/shard_map/all_to_all | solution.py:54
  17.5 8.5 %copy-start.14 = (bf16[4096,1024]{1,0:T(8,128)(2,1)S(1)}, bf16[4096,1024]{1,0:T(8,128)(2,1)}, u32[]{:S(2)}) copy-start(bf16[4096,1024]{1,0:T(8,128)(2,1)} %param.7) | copy-start | bytes 25165828
  17.5 8.5 %copy-start.15 = (bf16[512,4096]{1,0:T(8,128)(2,1)S(1)}, bf16[512,4096]{1,0:T(8,128)(2,1)}, u32[]{:S(2)}) copy-start(bf16[512,4096]{1,0:T(8,128)(2,1)} %param.6) | copy-start | bytes 12582916
  57.3 10.1 %copy-start.13 = (s32[4,4]{1,0:T(4,128)S(1)}, s32[4,4]{1,0:T(4,128)}, u32[]{:S(2)}) copy-start(s32[4,4]{1,0:T(4,128)} %param.8) | copy-start | bytes 196
  57.3 110.3 %all-to-all-start.1 = ((bf16[32,1,128,1024]{3,2,1,0:T(8,128)(2,1)}), bf16[32,1,128,1024]{3,2,1,0:T(8,128)(2,1)}, u32[]{:S(2)}, u32[]{:S(2)}) async-start(bf16[32,1,128,1024]{3,2,1,0:T(8,128)(2,1)} %fusion.3), calls=%async_computation.1 | async-start | bytes 16777216 | tf_op jit(solution)/shard_map/all_to_all | solution.py:60
  66.8 156.8 %all-reduce.4.cloned.1.call-start = ((), (), s32[]{:S(2)}) async-start(), calls=%async_computation.6 | async-start | bytes 1310720 | tf_op jit(solution)/shard_map/psum | solution.py:74
  176.4 2.8 copy-start.4
  176.8 2.4 copy-start.1
  176.8 46.8 %copy-start.12 = (s32[512]{0:T(512)S(1)}, s32[512]{0:T(512)}, u32[]{:S(2)}) copy-start(s32[512]{0:T(512)} %param.9) | copy-start | bytes 6148
  176.9 48.4 %copy-start.5 = (bf16[512,1024]{1,0:T(8,128)(2,1)S(1)}, bf16[512,1024]{1,0:T(8,128)(2,1)}, u32[]{:S(2)}) copy-start(bf16[512,1024]{1,0:T(8,128)(2,1)} %multiply_convert_fusion.1) | copy-start | bytes 3145732
  228.0 4.0 copy-start
  250.1 10.3 %copy-start.9 = (bf16[4,128,640]{2,1,0:T(8,128)(2,1)S(1)}, bf16[4,128,640]{2,1,0:T(8,128)(2,1)}, u32[]{:S(2)}) copy-start(bf16[4,128,640]{2,1,0:T(8,128)(2,1)} %all-reduce.4.cloned.1.call-done) | copy-start | bytes 1966084
  250.1 110.8 %all-to-all-start.2 = ((bf16[32,1,128,1024]{3,2,1,0:T(8,128)(2,1)}), bf16[32,1,128,1024]{3,2,1,0:T(8,128)(2,1)}, u32[]{:S(2)}, u32[]{:S(2)}) async-start(bf16[32,1,128,1024]{3,2,1,0:T(8,128)(2,1)} %bitcast.72), calls=%async_computation.2 | async-start | bytes 16777216 | tf_op jit(solution)/shard_map/all_to_all | solution.py:101
  260.2 254.1 %reduce-scatter.10.cloned.1.call-start = ((), (), s32[]{:S(2)}) async-start(), calls=%async_computation.9 | async-start | bytes 8650752
  264.2 1.3 copy-start.6
  373.4 4.6 copy-start.2
  376.6 1.4 copy-start.3
  385.6 2.9 copy-start.7
  385.6 4.5 copy-start.8
  388.3 9.8 %copy-start.10 = (bf16[512,1024]{1,0:T(8,128)(2,1)}, bf16[512,1024]{1,0:T(8,128)(2,1)S(1)}, u32[]{:S(2)}) copy-start(bf16[512,1024]{1,0:T(8,128)(2,1)S(1)} %fusion.7) | copy-start | bytes 3145732
  421.5 143.9 %reduce-scatter.6.cloned.1.call-start = ((), (), s32[]{:S(2)}) async-start(), calls=%async_computation.7 | async-start | bytes 5242880 | tf_op jit(solution)/shard_map/reduce_scatter | solution.py:134
  431.0 1.4 copy-start.11
  431.0 183.9 %reduce-scatter.8.cloned.1.call-start = ((), (), s32[]{:S(2)}) async-start(), calls=%async_computation.8 | async-start | bytes 5242880 | tf_op jit(solution)/shard_map/reduce_scatter | solution.py:135
Sparse Core Ops, SparseCore 0:
  181.9 41.6 all-reduce.3
  421.6 92.6 reduce-scatter.9
  517.3 48.0 reduce-scatter.5
  568.3 46.6 reduce-scatter.7
where the time goes:
time: 629 us; the launch traced here: 622 us
  waiting for transfers between devices  406 us (65%)
  matrix products  74.6 us (12%)
  local copies, waits for them, and re-layouts  56.5 us (9%)
  starting transfers between devices  29 us (5%)
  other arithmetic  24.7 us (4%)
  blocking collectives  16.9 us (3%)
  between operations  14.3 us (2%)
    all_to_all x1, waiting for transfers between devices, local(): lax.all_to_all(reply, 'dp', split_axis=0, concat_axis=0, tiled=True)  98.8 us
    all_to_all x1, waiting for transfers between devices, local(): lax.all_to_all(outgoing, 'dp', split_axis=0, concat_axis=0, tiled=True)  94.9 us
    unnamed x5, waiting for transfers between devices  71.6 us
    reduce_scatter x1, waiting for transfers between devices, local(): lax.psum_scatter(passage_back, 'mp', scatter_dimension=1, tiled=True)  49.5 us
    reduce_scatter x1, waiting for transfers between devices, local(): lax.psum_scatter(query_back, 'mp', scatter_dimension=1, tiled=True)  49 us
    psum x1, waiting for transfers between devices, local(): lax.psum(similarity_parts.astype(jnp.bfloat16), 'mp').astype(jnp.float32)  41.8 us
    unnamed x35, local copies, waits for them, and re-layouts  25.6 us
  transfers between devices with their start and end apart: 7, of which 6 were waited for; matrix products, arithmetic and copies ran while one was open for 7% of the time, Pallas kernels for 0%

commit v1 on v0

--- a/solution.py
+++ b/solution.py
@@ -11,6 +11,22 @@
     return (inverse[:, None] * (d_unit - unit_rows * inner[:, None])).astype(jnp.bfloat16)
 
 
+def to_pieces(blocks, row_groups, feature_groups):
+    count, rows, cols = blocks.shape
+    parts = blocks.reshape(
+        count, row_groups, rows // row_groups, feature_groups, cols // feature_groups
+    )
+    return parts.transpose(1, 3, 0, 2, 4).reshape(
+        row_groups * feature_groups, count, rows // row_groups, cols // feature_groups
+    )
+
+
+def from_pieces(pieces, row_groups, feature_groups):
+    _, count, rows, cols = pieces.shape
+    parts = pieces.reshape(row_groups, feature_groups, count, rows, cols)
+    return parts.transpose(2, 0, 3, 1, 4).reshape(count, row_groups * rows, feature_groups * cols)
+
+
 def local(query_hidden, passage_hidden, head_weight, neg_blocks, pos_ids):
     dp_count = lax.axis_size("dp")
     block_count, neg_count = neg_blocks.shape
@@ -19,8 +35,12 @@
     embed_width = head_weight.shape[1]
     cand_rows = (1 + neg_count) * block_rows
     request_count = block_count * neg_count
-    slot_depth = (request_count + dp_count - 1) // dp_count
-    slot_count = dp_count * slot_depth
+    total_blocks = dp_count * block_count
+    feature_groups = 4
+    row_groups = dp_count // feature_groups
+    piece_rows = block_rows // row_groups
+    piece_cols = embed_width // feature_groups
+    all_wanted = lax.all_gather(neg_blocks.reshape(request_count), "dp", tiled=True)
     query_embed = jnp.dot(query_hidden, head_weight, preferred_element_type=jnp.float32)
     passage_embed = jnp.dot(passage_hidden, head_weight, preferred_element_type=jnp.float32)
     query_sq, passage_sq = lax.psum(
@@ -38,29 +58,14 @@
     passage_norm = passage_unit.astype(jnp.bfloat16)
     query_blocks = query_norm.reshape(block_count, block_rows, embed_width)
     passage_blocks = passage_norm.reshape(block_count, block_rows, embed_width)
-    wanted = neg_blocks.reshape(-1)
-    owners = wanted // block_count
-    local_ids = wanted % block_count
-    request_order = jnp.arange(request_count, dtype=jnp.int32)
-    earlier_same = (owners[:, None] == owners[None, :]) & (
-        request_order[None, :] < request_order[:, None]
+    pieces = to_pieces(passage_blocks, row_groups, feature_groups)
+    held = lax.all_to_all(pieces, "dp", split_axis=0, concat_axis=0, tiled=True)
+    held = held.reshape(total_blocks, piece_rows, piece_cols)
+    reply = jnp.take(held, all_wanted, axis=0).reshape(
+        dp_count, request_count, piece_rows, piece_cols
     )
-    owner_rank = jnp.sum(earlier_same.astype(jnp.int32), axis=1)
-    slot_of = owners * slot_depth + owner_rank
-    slot_table = (slot_of[:, None] == jnp.arange(slot_count, dtype=jnp.int32)[None, :]).astype(
-        jnp.int32
-    )
-    requests = jnp.sum(slot_table * (local_ids + 1)[:, None], axis=0).reshape(dp_count, slot_depth)
-    asked = lax.all_to_all(requests, "dp", split_axis=0, concat_axis=0, tiled=True).reshape(
-        slot_count
-    )
-    live_slots = (asked > 0).astype(jnp.bfloat16)
-    picked = jnp.take(passage_blocks, jnp.maximum(asked - 1, 0), axis=0) * live_slots[:, None, None]
-    reply = picked.reshape(dp_count, slot_depth, block_rows, embed_width)
-    arrived = lax.all_to_all(reply, "dp", split_axis=0, concat_axis=0, tiled=True).reshape(
-        slot_count, block_rows, embed_width
-    )
-    fetched = jnp.take(arrived, slot_of, axis=0).reshape(
+    arrived = lax.all_to_all(reply, "dp", split_axis=0, concat_axis=0, tiled=True)
+    fetched = from_pieces(arrived, row_groups, feature_groups).reshape(
         block_count, neg_count, block_rows, embed_width
     )
     retrieved_documents = jnp.concatenate([passage_blocks[:, None], fetched], axis=1).reshape(
@@ -94,19 +99,19 @@
     neg_terms = (
         d_cand[:, block_rows:].reshape(request_count, block_rows, embed_width).astype(jnp.bfloat16)
     )
-    outgoing = (
-        jnp.zeros((slot_count, block_rows, embed_width), jnp.bfloat16).at[slot_of].set(neg_terms)
-    )
-    outgoing = outgoing.reshape(dp_count, slot_depth, block_rows, embed_width)
-    returned = lax.all_to_all(outgoing, "dp", split_axis=0, concat_axis=0, tiled=True).reshape(
-        slot_count, block_rows, embed_width
-    )
-    selector = (asked[None, :] - 1 == jnp.arange(block_count, dtype=jnp.int32)[:, None]).astype(
-        jnp.bfloat16
-    )
-    d_passage = own_terms + jnp.einsum(
-        "ls,sbe->lbe", selector, returned, preferred_element_type=jnp.float32
-    )
+    outgoing = to_pieces(neg_terms, row_groups, feature_groups)
+    returned = lax.all_to_all(outgoing, "dp", split_axis=0, concat_axis=0, tiled=True)
+    selector = (
+        all_wanted[None, :] == jnp.arange(total_blocks, dtype=jnp.int32)[:, None]
+    ).astype(jnp.bfloat16)
+    summed = jnp.dot(
+        selector,
+        returned.reshape(dp_count * request_count, piece_rows * piece_cols),
+        preferred_element_type=jnp.float32,
+    ).astype(jnp.bfloat16)
+    summed = summed.reshape(dp_count, block_count, piece_rows, piece_cols)
+    home = lax.all_to_all(summed, "dp", split_axis=0, concat_axis=0, tiled=True)
+    d_passage = own_terms + from_pieces(home, row_groups, feature_groups).astype(jnp.float32)
     d_passage = d_passage.reshape(row_count, embed_width)
     query_inner, passage_inner = lax.psum(
         (jnp.sum(query_unit * d_query, axis=1), jnp.sum(passage_unit * d_passage, axis=1)), "mp"

time: 629 us -> 567 us (0.901)
  waiting for transfers between devices: 406 us -> 265 us
  blocking collectives: 16.9 us -> 99.1 us
  local copies, waits for them, and re-layouts: 56.5 us -> 74.9 us
  matrix products: 74.6 us -> 64.4 us
  other arithmetic: 24.7 us -> 17.8 us
  starting transfers between devices: 29 us -> 22.7 us
    all_to_all x2, waiting for transfers between devices: 94.9 us -> 11.2 us  [the longest x1 11.2 us: local(): home = lax.all_to_all(summed, 'dp', split_axis=0, concat_axis=0, tiled=True)]
    all_to_all x0 -> x1, blocking collectives: none -> 60.5 us  [local(): lax.all_to_all(outgoing, 'dp', split_axis=0, concat_axis=0, tiled=True)]
    all_to_all x1, waiting for transfers between devices: 98.8 us -> 48.4 us  [local(): lax.all_to_all(reply, 'dp', split_axis=0, concat_axis=0, tiled=True)]
    unnamed x0 -> x1, blocking collectives: none -> 20.6 us
    convert_element_type x0 -> x4, local copies, waits for them, and re-layouts: none -> 17.2 us  [the longest x2 10.8 us: local(): d_cand[:, block_rows:].reshape(request_count, block_rows, embed_width)]
    another operation x0 -> x3, local copies, waits for them, and re-layouts: none -> 11.7 us  [the longest x1 7.71 us: local(): from_pieces(arrived, row_groups, feature_groups)]
    dot_general x1, matrix products: 12.4 us -> 0.74 us  [local(): jnp.dot(selector, returned.reshape(dp_count * request_count, piece_rows *...]
    scatter x1 -> x0, local copies, waits for them, and re-layouts: 11 us -> none  [local(): jnp.zeros((slot_count, block_rows, embed_width), jnp.bfloat16).at[slot_of]]
  transfers between devices with their start and end apart: 7 -> 7, of which waited for: 6 -> 6; matrix products, arithmetic and copies ran while one was open for 7% -> 5% of each run, Pallas kernels for 0% -> 0%
where the time goes in v1:
time: 567 us; the launch traced here: 558 us
  waiting for transfers between devices  265 us (47%)
  blocking collectives  99.1 us (17%)
  local copies, waits for them, and re-layouts  74.9 us (13%)
  matrix products  64.4 us (11%)
  starting transfers between devices  22.7 us (4%)
  other arithmetic  17.8 us (3%)
  between operations  14.9 us (3%)
    unnamed x5, waiting for transfers between devices  67 us
    all_to_all x1, blocking collectives, local(): lax.all_to_all(outgoing, 'dp', split_axis=0, concat_axis=0, tiled=True)  60.5 us
    reduce_scatter x1, waiting for transfers between devices, local(): lax.psum_scatter(passage_back, 'mp', scatter_dimension=1, tiled=True)  49.5 us
    reduce_scatter x1, waiting for transfers between devices, local(): lax.psum_scatter(query_back, 'mp', scatter_dimension=1, tiled=True)  49 us
    all_to_all x1, waiting for transfers between devices, local(): lax.all_to_all(reply, 'dp', split_axis=0, concat_axis=0, tiled=True)  48.4 us
    psum x1, waiting for transfers between devices, local(): lax.psum(similarity_parts.astype(jnp.bfloat16), 'mp').astype(jnp.float32)  39.4 us
    unnamed x38, local copies, waits for them, and re-layouts  30.2 us
    unnamed x1, blocking collectives  20.6 us
  transfers between devices with their start and end apart: 7, of which 6 were waited for; matrix products, arithmetic and copies ran while one was open for 5% of the time, Pallas kernels for 0%

profile of v1, /device:TPU:1, one launch (start us, length us, event | category | flops | bytes accessed | tf_op | source)
XLA Modules:
  0.0 558.4 jit_solution(768447223770968793)
XLA Ops:
  7.2 10.7 %multiply_reduce_fusion.1 = (f32[512]{0:T(512)S(1)}, f32[512,1024]{1,0:T(8,128)}) fusion(bf16[512,4096]{1,0:T(8,128)(2,1)} %param.5, bf16[4096,1024]{1,0:T(8,128)(2,1)} %param.7), kind=kOutput, calls=%fused_computation.22 | convolution fusion | flops 4296015360 | bytes 14682112 | tf_op jit(solution)/shard_map/dot_general | solution.py:44
  17.9 4.6 multiply_reduce_fusion
  22.4 10.6 %all-reduce.2 = (f32[512]{0:T(512)S(1)}, f32[512]{0:T(512)S(1)}) all-reduce(f32[512]{0:T(512)S(1)} %get-tuple-element.26, f32[512]{0:T(512)S(1)} %get-tuple-element.28), channel_id=1, replica_groups=mesh['dp'=32,'mp'=4] {'mp'}, use_global_device_ids=true, to_apply=%region_3.0 | all-reduce | flops 1024 | bytes 8192 | tf_op jit(solution)/shard_map/psum | solution.py:46
  33.2 1.6 reshape_reshape.6
  34.8 2.4 copy.25
  37.2 9.8 %all-to-all-start = ((bf16[32,4,16,256]{3,2,1,0:T(8,128)(2,1)}), bf16[32,4,16,256]{3,2,1,0:T(8,128)(2,1)S(1)}, u32[]{:S(2)}, u32[]{:S(2)}) async-start(bf16[32,4,16,256]{3,2,1,0:T(8,128)(2,1)} %bitcast.80), calls=%async_computation | async-start | bytes 2097152 | tf_op jit(solution)/shard_map/all_to_all | solution.py:62
  48.6 20.6 %all-reduce = s32[512]{0:T(512)S(1)} all-reduce(s32[512]{0:T(512)S(1)} %dynamic-update-slice), channel_id=1, replica_groups=mesh['dp'=32,'mp'=4] {'dp'}, use_global_device_ids=true, to_apply=%add | all-reduce | flops 512 | bytes 4096
  69.4 3.4 gather_fusion
  72.8 3.9 broadcast_select_fusion
  76.7 8.3 %all-to-all-start.1 = ((bf16[32,16,16,256]{3,2,1,0:T(8,128)(2,1)}), bf16[32,16,16,256]{3,2,1,0:T(8,128)(2,1)}, u32[]{:S(2)}, u32[]{:S(2)}) async-start(bf16[32,16,16,256]{3,2,1,0:T(8,128)(2,1)} %broadcast_select_fusion), calls=%async_computation.1 | async-start | bytes 8388608 | tf_op jit(solution)/shard_map/all_to_all | solution.py:67
  85.5 1.8 multiply_convert_fusion.1
  87.3 48.4 %all-to-all-done.1 = bf16[32,16,16,256]{3,2,1,0:T(8,128)(2,1)} async-done(((bf16[32,16,16,256]{3,2,1,0:T(8,128)(2,1)}), bf16[32,16,16,256]{3,2,1,0:T(8,128)(2,1)}, u32[]{:S(2)}, u32[]{:S(2)}) %all-to-all-start.1) | async-done | bytes 4194336 | tf_op jit(solution)/shard_map/all_to_all | solution.py:67
  135.7 9.5 %copy.26 = bf16[16,8,16,4,256]{4,3,2,1,0:T(4,128)(2,1)} copy(bf16[16,8,16,4,256]{4,2,0,3,1:T(8,128)(2,1)} %bitcast.9) | data formatting | bytes 8388608 | tf_op jit(solution)/shard_map/transpose | solution.py:27
  145.3 7.7 %reshape_reshape.7 = bf16[4,4,128,1024]{3,2,1,0:T(8,128)(2,1)} reshape(bf16[16,8,16,4,256]{4,3,2,1,0:T(4,128)(2,1)} %copy.26) | data formatting | bytes 8388608 | tf_op jit(solution)/shard_map/reshape;reshape | solution.py:68
  153.0 2.9 pad_maximum_fusion
  155.9 2.4 copy-done.1
  158.3 2.7 convolution_convert_fusion.3
  161.0 39.4 %all-reduce.5.cloned.1.call-done = bf16[4,128,640]{2,1,0:T(8,128)(2,1)} async-done(((bf16[4,128,640]{2,1,0:T(8,128)(2,1)}), bf16[4,128,640]{2,1,0:T(8,128)(2,1)}) %all-reduce.5.cloned.1.call-update) | async-done | bytes 655376 | tf_op jit(solution)/shard_map/psum | solution.py:79
  200.3 1.6 fusion.8
  201.9 2.7 fusion.10
  204.6 4.0 copy-done
  208.6 2.6 slice.15
  211.2 7.9 %convert_element_type.71 = bf16[16,8,16,4,256]{4,3,2,1,0:T(4,128)(2,1)} reshape(bf16[4,512,1024]{2,1,0:T(8,128)(2,1)} %slice.15) | data formatting | bytes 8388608 | tf_op jit(solution)/shard_map/convert_element_type | solution.py:100
  219.1 3.0 copy.29
  222.1 60.5 %all_to_all.20 = bf16[32,16,16,256]{3,2,1,0:T(8,128)(2,1)S(1)} all-to-all(bf16[32,16,16,256]{3,2,1,0:T(8,128)(2,1)S(1)} %bitcast.73), channel_id=1, replica_groups=mesh['dp'=32,'mp'=4] {'dp'}, dimensions={0} | all-to-all | bytes 8388608 | tf_op jit(solution)/shard_map/all_to_all | solution.py:103
  282.6 2.2 copy.35
  285.5 1.2 copy.36
  286.8 4.0 all-to-all-start.3
  290.8 4.2 fusion.11
  295.0 1.3 copy-done.6
  296.7 11.2 %all-to-all-done.3 = bf16[32,4,16,256]{3,2,1,0:T(8,128)(2,1)S(1)} async-done(((bf16[32,4,16,256]{3,2,1,0:T(8,128)(2,1)}), bf16[32,4,16,256]{3,2,1,0:T(8,128)(2,1)S(1)}, u32[]{:S(2)}, u32[]{:S(2)}) %all-to-all-start.3) | async-done | bytes 1048608 | tf_op jit(solution)/shard_map/all_to_all | solution.py:113
  308.2 3.1 copy.30
  311.3 3.3 reshape.83
  314.6 2.6 slice_add_fusion
  317.2 1.3 copy-done.3
  319.0 7.4 %all-reduce.1 = (f32[512]{0:T(512)S(1)}, f32[512]{0:T(512)S(1)}) all-reduce(f32[512]{0:T(512)S(1)} %fusion.4, f32[512]{0:T(512)S(1)} %fusion.1), channel_id=1, replica_groups=mesh['dp'=32,'mp'=4] {'mp'}, use_global_device_ids=true, to_apply=%region_8.9 | all-reduce | flops 1024 | bytes 8192 | tf_op jit(solution)/shard_map/psum | solution.py:116
  326.5 2.7 fusion.6
  329.9 8.2 %fusion.12 = f32[1024,4096]{1,0:T(8,128)} fusion(bf16[512,1024]{1,0:T(8,128)(2,1)S(1)} %fusion.6, bf16[512,4096]{1,0:T(8,128)(2,1)S(1)} %copy-done.7), kind=kOutput, calls=%fused_computation.42 | convolution fusion | flops 4294967296 | bytes 22020096 | tf_op jit(solution)/shard_map/dot_general | solution.py:122
  338.5 1.0 copy-done.8
  339.5 11.4 %fusion = bf16[4096,1024]{0,1:T(8,128)(2,1)} fusion(f32[1024,4096]{1,0:T(8,128)} %fusion.12, bf16[512,1024]{1,0:T(8,128)(2,1)S(1)} %fusion.3, bf16[512,4096]{1,0:T(8,128)(2,1)} %param.6), kind=kOutput, calls=%fused_computation.2 | convolution fusion | flops 4303355904 | bytes 30408704 | tf_op jit(solution)/shard_map/dot_general | solution.py:125
  350.8 12.0 %copy.33 = bf16[4096,1024]{1,0:T(8,128)(2,1)} copy(bf16[4096,1024]{0,1:T(8,128)(2,1)} %fusion) | data formatting | bytes 16777216
  362.9 9.5 %convolution_convert_fusion.1 = bf16[512,4096]{1,0:T(8,128)(2,1)} fusion(bf16[512,1024]{1,0:T(8,128)(2,1)S(1)} %fusion.6, bf16[4096,1024]{1,0:T(8,128)(2,1)} %param.7), kind=kOutput, calls=%fused_computation.5 | convolution fusion | flops 4297064448 | bytes 13631488 | tf_op jit(solution)/shard_map/dot_general | solution.py:132
  372.4 1.2 copy-done.9
  373.6 9.9 %convolution_convert_fusion = bf16[512,4096]{1,0:T(8,128)(2,1)} fusion(bf16[512,1024]{1,0:T(8,128)(2,1)S(1)} %copy-done.9, bf16[4096,1024]{1,0:T(8,128)(2,1)} %param.7), kind=kOutput, calls=%fused_computation.4 | convolution fusion | flops 4297064448 | bytes 13631488 | tf_op jit(solution)/shard_map/dot_general | solution.py:135
  384.1 67.0 %reduce-scatter.10.cloned.1.call-done = bf16[128,1024]{1,0:T(8,128)(2,1)} async-done(((bf16[4096,1024]{1,0:T(8,128)(2,1)}), bf16[128,1024]{1,0:T(8,128)(2,1)}) %reduce-scatter.10.cloned.1.call-update) | async-done | bytes 262160
  451.1 1.1 copy.34
  453.1 49.0 %reduce-scatter.6.cloned.1.call-done = bf16[512,1024]{1,0:T(8,128)(2,1)} async-done(((bf16[512,4096]{1,0:T(8,128)(2,1)}), bf16[512,1024]{1,0:T(8,128)(2,1)}) %reduce-scatter.6.cloned.1.call-update) | async-done | bytes 1048592 | tf_op jit(solution)/shard_map/reduce_scatter | solution.py:139
  502.1 49.5 %reduce-scatter.8.cloned.1.call-done = bf16[512,1024]{1,0:T(8,128)(2,1)} async-done(((bf16[512,4096]{1,0:T(8,128)(2,1)}), bf16[512,1024]{1,0:T(8,128)(2,1)}) %reduce-scatter.8.cloned.1.call-update) | async-done | bytes 1048592 | tf_op jit(solution)/shard_map/reduce_scatter | solution.py:140
  (50 shorter events, 6.4 us)
Async XLA Ops:
  7.2 10.7 %copy-start.12 = (bf16[4096,1024]{1,0:T(8,128)(2,1)S(1)}, bf16[4096,1024]{1,0:T(8,128)(2,1)}, u32[]{:S(2)}) copy-start(bf16[4096,1024]{1,0:T(8,128)(2,1)} %param.7) | copy-start | bytes 25165828
  7.2 10.7 %copy-start.13 = (bf16[512,4096]{1,0:T(8,128)(2,1)S(1)}, bf16[512,4096]{1,0:T(8,128)(2,1)}, u32[]{:S(2)}) copy-start(bf16[512,4096]{1,0:T(8,128)(2,1)} %param.6) | copy-start | bytes 12582916
  33.2 4.0 copy-start.5
  34.8 12.2 %copy-start.11 = (s32[4,4]{1,0:T(4,128)S(1)}, s32[4,4]{1,0:T(4,128)}, u32[]{:S(2)}) copy-start(s32[4,4]{1,0:T(4,128)} %param.8) | copy-start | bytes 196
  34.8 12.3 %copy-start.14 = (u32[128]{0:T(128)S(1)}, u32[128]{0:T(128)}, u32[]{:S(2)}) copy-start(u32[128]{0:T(128)} %constant.28) | copy-start | bytes 1540
  37.2 32.1 %all-to-all-start = ((bf16[32,4,16,256]{3,2,1,0:T(8,128)(2,1)}), bf16[32,4,16,256]{3,2,1,0:T(8,128)(2,1)S(1)}, u32[]{:S(2)}, u32[]{:S(2)}) async-start(bf16[32,4,16,256]{3,2,1,0:T(8,128)(2,1)} %bitcast.80), calls=%async_computation | async-start | bytes 2097152 | tf_op jit(solution)/shard_map/all_to_all | solution.py:62
  76.7 59.0 %all-to-all-start.1 = ((bf16[32,16,16,256]{3,2,1,0:T(8,128)(2,1)}), bf16[32,16,16,256]{3,2,1,0:T(8,128)(2,1)}, u32[]{:S(2)}, u32[]{:S(2)}) async-start(bf16[32,16,16,256]{3,2,1,0:T(8,128)(2,1)} %broadcast_select_fusion), calls=%async_computation.1 | async-start | bytes 8388608 | tf_op jit(solution)/shard_map/all_to_all | solution.py:67
  85.0 115.3 %all-reduce.5.cloned.1.call-start = ((), (), s32[]{:S(2)}) async-start(), calls=%async_computation.7 | async-start | bytes 1310720 | tf_op jit(solution)/shard_map/psum | solution.py:79
  155.9 2.4 copy-start.1
  158.3 42.0 %copy-start.10 = (s32[512]{0:T(512)S(1)}, s32[512]{0:T(512)}, u32[]{:S(2)}) copy-start(s32[512]{0:T(512)} %param.9) | copy-start | bytes 6148
  204.6 4.0 copy-start
  286.8 21.1 %all-to-all-start.3 = ((bf16[32,4,16,256]{3,2,1,0:T(8,128)(2,1)}), bf16[32,4,16,256]{3,2,1,0:T(8,128)(2,1)S(1)}, u32[]{:S(2)}, u32[]{:S(2)}) async-start(bf16[32,4,16,256]{3,2,1,0:T(8,128)(2,1)} %bitcast.81), calls=%async_computation.3 | async-start | bytes 2097152 | tf_op jit(solution)/shard_map/all_to_all | solution.py:113
  290.8 160.3 %reduce-scatter.10.cloned.1.call-start = ((), (), s32[]{:S(2)}) async-start(), calls=%async_computation.10 | async-start | bytes 8650752
  290.8 5.5 copy-start.2
  295.0 1.3 copy-start.6
  317.2 1.3 copy-start.3
  326.4 3.4 copy-start.7
  329.9 8.2 %copy-start.4 = (f32[4,128,1024]{2,1,0:T(8,128)S(1)}, f32[4,128,1024]{2,1,0:T(8,128)}, u32[]{:S(2)}) copy-start(f32[4,128,1024]{2,1,0:T(8,128)} %copy-done.3) | copy-start | bytes 6291460
  338.5 1.0 copy-start.8
  362.8 139.3 %reduce-scatter.6.cloned.1.call-start = ((), (), s32[]{:S(2)}) async-start(), calls=%async_computation.8 | async-start | bytes 5242880 | tf_op jit(solution)/shard_map/reduce_scatter | solution.py:139
  372.3 1.3 copy-start.9
  372.4 179.3 %reduce-scatter.8.cloned.1.call-start = ((), (), s32[]{:S(2)}) async-start(), calls=%async_computation.9 | async-start | bytes 5242880 | tf_op jit(solution)/shard_map/reduce_scatter | solution.py:140
Sparse Core Ops, SparseCore 0:
  161.1 39.1 all-reduce.4
  362.9 88.0 reduce-scatter.9
  454.0 48.0 reduce-scatter.5
  505.0 46.6 reduce-scatter.7

commit v2 on v1

--- a/solution.py
+++ b/solution.py
@@ -1,6 +1,8 @@
 import jax
 import jax.numpy as jnp
 from jax import lax
+from jax.experimental import pallas as pl
+from jax.experimental.pallas import tpu as pltpu
 from jax.sharding import PartitionSpec as P
 
 logit_divisor = 0.02
@@ -9,6 +11,372 @@
 
 def back_norm(inverse, unit_rows, d_unit, inner):
     return (inverse[:, None] * (d_unit - unit_rows * inner[:, None])).astype(jnp.bfloat16)
+
+
+MESH = pl.DeviceIdType.MESH
+ROW_CONTRACT = (((0,), (0,)), ((), ()))
+COL_CONTRACT = (((1,), (1,)), ((), ()))
+VMEM_LIMIT = 66 * 1024 * 1024 - 4 * 1024 * 1024
+
+
+def greet(partners):
+    barrier = pltpu.get_barrier_semaphore()
+    for partner in partners:
+        pl.semaphore_signal(barrier, 1, device_id=partner, device_id_type=MESH)
+    pl.semaphore_wait(barrier, len(partners))
+
+
+def remote(src, dst, send_sem, recv_sem, partner):
+    return pltpu.make_async_remote_copy(
+        src_ref=src,
+        dst_ref=dst,
+        send_sem=send_sem,
+        recv_sem=recv_sem,
+        device_id=partner,
+        device_id_type=MESH,
+    )
+
+
+def depth_partner(k):
+    return {"mp": lax.rem(lax.axis_index("mp") + k, 4)}
+
+
+def head_load(head_hbm, head, load_sem, k):
+    width = head.shape[1]
+    owner = lax.rem(lax.axis_index("mp") + k, 4)
+    return pltpu.make_async_copy(
+        head_hbm.at[pl.ds(pl.multiple_of(owner * width, width), width)], head.at[k], load_sem.at[k]
+    )
+
+
+def hidden_send(part, landed, send_sem, recv_sem, k):
+    return remote(
+        part.at[k], landed.at[k - 1], send_sem.at[k - 1], recv_sem.at[k - 1], depth_partner(k)
+    )
+
+
+DEPTH_ORDER = (2, 1, 3, 0)
+
+
+def hidden_parts(grad, head_hbm, head, part, landed, load_sem, send_sem, recv_sem):
+    for k in DEPTH_ORDER:
+        head_load(head_hbm, head, load_sem, k).wait()
+        half = grad.shape[0] // 2
+
+        @pl.loop(0, 2)
+        def _(i):
+            rows = pl.ds(pl.multiple_of(i * half, half), half)
+            part[k, rows] = lax.dot_general(
+                grad[rows], head[k], COL_CONTRACT, preferred_element_type=jnp.float32
+            ).astype(jnp.bfloat16)
+
+        if k:
+            hidden_send(part, landed, send_sem, recv_sem, k).start()
+
+
+def hidden_sum(part, landed, send_sem, recv_sem, out):
+    for k in (1, 3, 2):
+        hidden_send(part, landed, send_sem, recv_sem, k).wait_recv()
+    rows_step = 64
+
+    @pl.loop(0, out.shape[0] // rows_step)
+    def _(i):
+        rows = pl.ds(pl.multiple_of(i * rows_step, rows_step), rows_step)
+        total = part[0, rows].astype(jnp.float32)
+        for k in range(3):
+            total = total + landed[k, rows].astype(jnp.float32)
+        out[rows] = total.astype(jnp.bfloat16)
+
+    for k in (1, 3, 2):
+        hidden_send(part, landed, send_sem, recv_sem, k).wait_send()
+
+
+def hidden_kernel(grad, head_hbm, out, head, part, landed, load_sem, send_sem, recv_sem):
+    for k in DEPTH_ORDER:
+        head_load(head_hbm, head, load_sem, k).start()
+    greet([depth_partner(k) for k in (1, 2, 3)])
+    hidden_parts(grad, head_hbm, head, part, landed, load_sem, send_sem, recv_sem)
+    hidden_sum(part, landed, send_sem, recv_sem, out)
+
+
+def hidden_grad(grad, head_weight):
+    rows, width = grad.shape
+    return pl.pallas_call(
+        hidden_kernel,
+        out_shape=jax.ShapeDtypeStruct((rows, width), jnp.bfloat16),
+        in_specs=[pl.BlockSpec(memory_space=pltpu.VMEM), pl.BlockSpec(memory_space=pl.ANY)],
+        out_specs=pl.BlockSpec(memory_space=pltpu.VMEM),
+        scratch_shapes=[
+            pltpu.VMEM((4, width, width), jnp.bfloat16),
+            pltpu.VMEM((4, rows, width), jnp.bfloat16),
+            pltpu.VMEM((3, rows, width), jnp.bfloat16),
+            pltpu.SemaphoreType.DMA((4,)),
+            pltpu.SemaphoreType.DMA((3,)),
+            pltpu.SemaphoreType.DMA((3,)),
+        ],
+        compiler_params=pltpu.CompilerParams(
+            collective_id=1, has_side_effects=True, vmem_limit_bytes=32 * 1024 * 1024
+        ),
+        name="hidden_grad",
+    )(grad, head_weight)
+
+
+def place():
+    dp = lax.axis_index("dp")
+    return lax.div(dp, 8), lax.rem(lax.div(dp, 2), 4), lax.rem(dp, 2)
+
+
+def at(y, x, core):
+    return {"dp": y * 8 + x * 2 + core}
+
+
+def tail_kernel(
+    d_query,
+    d_passage,
+    query_hbm,
+    passage_hbm,
+    head_hbm,
+    weight_out,
+    hidden_out,
+    head,
+    query,
+    passage,
+    summed,
+    sibling_in,
+    pair,
+    first_in,
+    second_out,
+    second_in,
+    part,
+    landed,
+    load_sem,
+    hidden_load_sem,
+    depth_send,
+    depth_recv,
+    core_send,
+    core_recv,
+    first_send,
+    first_recv,
+    second_send,
+    second_recv,
+):
+    y, x, core = place()
+    wide = query.shape[1]
+    rows = weight_out.shape[0]
+    half = weight_out.shape[1] // 2
+
+    def chunk_of(i):
+        return lax.rem(y + 1 + lax.div(i, 2), 4) * 2 + lax.rem(lax.div(x, 2) + 1 + i, 2)
+
+    def hidden_loads(i, slot):
+        columns = pl.ds(pl.multiple_of(chunk_of(i) * wide, wide), wide)
+        return (
+            pltpu.make_async_copy(
+                query_hbm.at[:, columns], query.at[slot], hidden_load_sem.at[0, slot]
+            ),
+            pltpu.make_async_copy(
+                passage_hbm.at[:, columns], passage.at[slot], hidden_load_sem.at[1, slot]
+            ),
+        )
+
+    for k in DEPTH_ORDER:
+        head_load(head_hbm, head, load_sem, k).start()
+    for copy in hidden_loads(0, 0) + hidden_loads(1, 1):
+        copy.start()
+    greet(
+        [depth_partner(k) for k in (1, 2, 3)]
+        + [at(y, x, 1 - core)]
+        + [at(lax.rem(y + k, 4), x, core) for k in (1, 2, 3)]
+        + [at(y, lax.rem(x + k, 4), core) for k in (1, 2, 3)]
+    )
+    hidden_parts(d_passage, head_hbm, head, part, landed, load_sem, depth_send, depth_recv)
+
+    def core_copy(chip):
+        return remote(
+            summed.at[chip, 1 - core],
+            sibling_in.at[chip],
+            core_send.at[chip],
+            core_recv.at[chip],
+            at(y, x, 1 - core),
+        )
+
+    def first_x(chip):
+        to_y, to_x = lax.div(chip, 4), lax.rem(chip, 4)
+        k = lax.rem(to_x - x + 4, 4)
+        slot = lax.rem(k + 3, 4)
+        return k, remote(
+            pair.at[chip, 0],
+            first_in.at[0, slot, to_y],
+            first_send.at[0, chip],
+            first_recv.at[0, slot, to_y],
+            at(y, to_x, core),
+        )
+
+    def first_y(chip):
+        to_y, to_x = lax.div(chip, 4), lax.rem(chip, 4)
+        k = lax.rem(to_y - y + 4, 4)
+        slot = lax.rem(k + 3, 4)
+        return k, remote(
+            pair.at[chip, 1],
+            first_in.at[1, slot, to_x],
+            first_send.at[1, chip],
+            first_recv.at[1, slot, to_x],
+            at(to_y, x, core),
+        )
+
+    def produce(i):
+        slot = lax.rem(i, 2)
+        for copy in hidden_loads(i, slot):
+            copy.wait()
+        chunk = chunk_of(i)
+        for j in range(2):
+            columns = slice(j * 2 * rows, (j + 1) * 2 * rows)
+            total = lax.dot_general(
+                query[slot, :, columns], d_query[...], ROW_CONTRACT, preferred_element_type=jnp.float32
+            ) + lax.dot_general(
+                passage[slot, :, columns],
+                d_passage[...],
+                ROW_CONTRACT,
+                preferred_element_type=jnp.float32,
+            )
+            summed[chunk * 2 + j] = total.astype(jnp.bfloat16).reshape(2, rows, 2 * half)
+            core_copy(chunk * 2 + j).start()
+
+        @pl.when(i < 6)
+        def _():
+            for copy in hidden_loads(i + 2, slot):
+                copy.start()
+
+    def combine(i):
+        for j in range(2):
+            chip = chunk_of(i) * 2 + j
+            core_copy(chip).wait_recv()
+            total = (
+                summed[chip, core].astype(jnp.float32) + sibling_in[chip].astype(jnp.float32)
+            ).astype(jnp.bfloat16)
+            pair[chip, 0] = total[:, :half]
+            pair[chip, 1] = total[:, half:]
+            for first in (first_x, first_y):
+                k, copy = first(chip)
+
+                @pl.when(k != 0)
+                def _():
+                    copy.start()
+
+    @pl.loop(0, 9)
+    def _(i):
+        @pl.when(i < 8)
+        def _():
+            produce(i)
+
+        @pl.when(i > 0)
+        def _():
+            combine(i - 1)
+
+    def first_arrival(side, k, other):
+        return remote(
+            first_in.at[side, k, other],
+            first_in.at[side, k, other],
+            first_send.at[side, 0],
+            first_recv.at[side, k, other],
+            at(y, x, 1 - core),
+        )
+
+    def gathered(side, other):
+        chip = other * 4 + x if side == 0 else y * 4 + other
+        total = pair[chip, side].astype(jnp.float32)
+        for k in range(3):
+            first_arrival(side, k, other).wait_recv()
+            total = total + first_in[side, k, other].astype(jnp.float32)
+        return total
+
+    def second_copy(side, k):
+        if side == 0:
+            partner = at(lax.rem(y + k, 4), x, core)
+        else:
+            partner = at(y, lax.rem(x + k, 4), core)
+        return remote(
+            second_out.at[side, k - 1],
+            second_in.at[side, k - 1],
+            second_send.at[side, k - 1],
+            second_recv.at[side, k - 1],
+            partner,
+        )
+
+    for k in (1, 2, 3):
+        for side in range(2):
+            base = y if side == 0 else x
+            second_out[side, k - 1] = gathered(side, lax.rem(base + k, 4)).astype(jnp.bfloat16)
+            second_copy(side, k).start()
+    for side in range(2):
+        weight_out[:, side * half : (side + 1) * half] = gathered(side, y if side == 0 else x)
+    for side in range(2):
+        for k in (1, 2, 3):
+            second_copy(side, k).wait_recv()
+            weight_out[:, side * half : (side + 1) * half] += second_in[side, k - 1].astype(
+                jnp.float32
+            )
+    hidden_sum(part, landed, depth_send, depth_recv, hidden_out)
+
+    @pl.loop(0, 16)
+    def _(chip):
+        core_copy(chip).wait_send()
+        for first in (first_x, first_y):
+            k, copy = first(chip)
+
+            @pl.when(k != 0)
+            def _():
+                copy.wait_send()
+
+    for side in range(2):
+        for k in (1, 2, 3):
+            second_copy(side, k).wait_send()
+
+
+def tail(d_query, d_passage, query_hidden, passage_hidden, head_weight):
+    rows, width = d_query.shape
+    hidden = head_weight.shape[0]
+    share = hidden // 32
+    bf16 = jnp.bfloat16
+    vmem = pl.BlockSpec(memory_space=pltpu.VMEM)
+    hbm = pl.BlockSpec(memory_space=pl.ANY)
+    dma = pltpu.SemaphoreType.DMA
+    return pl.pallas_call(
+        tail_kernel,
+        out_shape=(
+            jax.ShapeDtypeStruct((share, width), jnp.float32),
+            jax.ShapeDtypeStruct((rows, width), bf16),
+        ),
+        in_specs=[vmem, vmem, hbm, hbm, hbm],
+        out_specs=(vmem, vmem),
+        scratch_shapes=[
+            pltpu.VMEM((4, width, width), bf16),
+            pltpu.VMEM((2, rows, 4 * share), bf16),
+            pltpu.VMEM((2, rows, 4 * share), bf16),
+            pltpu.VMEM((16, 2, share, width), bf16),
+            pltpu.VMEM((16, share, width), bf16),
+            pltpu.VMEM((16, 2, share, width // 2), bf16),
+            pltpu.VMEM((2, 3, 4, share, width // 2), bf16),
+            pltpu.VMEM((2, 3, share, width // 2), bf16),
+            pltpu.VMEM((2, 3, share, width // 2), bf16),
+            pltpu.VMEM((4, rows, width), bf16),
+            pltpu.VMEM((3, rows, width), bf16),
+            dma((4,)),
+            dma((2, 2)),
+            dma((3,)),
+            dma((3,)),
+            dma((16,)),
+            dma((16,)),
+            dma((2, 16)),
+            dma((2, 3, 4)),
+            dma((2, 3)),
+            dma((2, 3)),
+        ],
+        compiler_params=pltpu.CompilerParams(
+            collective_id=2, has_side_effects=True, vmem_limit_bytes=VMEM_LIMIT
+        ),
+        name="tail",
+    )(d_query, d_passage, query_hidden, passage_hidden, head_weight)
 
 
 def to_pieces(blocks, row_groups, feature_groups):
@@ -113,37 +481,19 @@
     home = lax.all_to_all(summed, "dp", split_axis=0, concat_axis=0, tiled=True)
     d_passage = own_terms + from_pieces(home, row_groups, feature_groups).astype(jnp.float32)
     d_passage = d_passage.reshape(row_count, embed_width)
-    query_inner, passage_inner = lax.psum(
-        (jnp.sum(query_unit * d_query, axis=1), jnp.sum(passage_unit * d_passage, axis=1)), "mp"
-    )
+    query_inner = lax.psum(jnp.sum(query_unit * d_query, axis=1), "mp")
+    passage_inner = lax.psum(jnp.sum(passage_unit * d_passage, axis=1), "mp")
     d_query_embed = back_norm(query_inv, query_unit, d_query, query_inner)
     d_passage_embed = back_norm(passage_inv, passage_unit, d_passage, passage_inner)
-    contract = (((0,), (0,)), ((), ()))
-    query_part = lax.dot_general(
-        query_hidden, d_query_embed, contract, preferred_element_type=jnp.float32
-    )
-    passage_part = lax.dot_general(
-        passage_hidden, d_passage_embed, contract, preferred_element_type=jnp.float32
-    )
-    grad_weight = lax.psum_scatter(
-        (query_part + passage_part).astype(jnp.bfloat16), "dp", scatter_dimension=0, tiled=True
-    ).astype(jnp.float32)
-    transpose_dims = (((1,), (1,)), ((), ()))
-    query_back = lax.dot_general(
-        d_query_embed, head_weight, transpose_dims, preferred_element_type=jnp.float32
-    ).astype(jnp.bfloat16)
-    passage_back = lax.dot_general(
-        d_passage_embed, head_weight, transpose_dims, preferred_element_type=jnp.float32
-    ).astype(jnp.bfloat16)
-    query_grad, passage_grad = (
-        lax.psum_scatter(query_back, "mp", scatter_dimension=1, tiled=True).astype(jnp.float32),
-        lax.psum_scatter(passage_back, "mp", scatter_dimension=1, tiled=True).astype(jnp.float32),
+    query_grad = hidden_grad(d_query_embed, head_weight)
+    grad_weight, passage_grad = tail(
+        d_query_embed, d_passage_embed, query_hidden, passage_hidden, head_weight
     )
     return (
         losses.reshape(row_count),
         grad_weight,
-        query_grad.astype(jnp.bfloat16),
-        passage_grad.astype(jnp.bfloat16),
+        query_grad,
+        passage_grad,
     )
 
 

time: 567 us -> 459 us (0.81)
  waiting for transfers between devices: 265 us -> 100 us
  Pallas kernels: 0 us -> 107 us
  matrix products: 64.4 us -> 24.4 us
  local copies, waits for them, and re-layouts: 74.9 us -> 64.9 us
    pallas_call x0 -> x2, Pallas kernels: none -> 107 us  [the longest x1 55.2 us: tail(): pl.pallas_call(tail_kernel, out_shape=(jax.ShapeDtypeStruct((share, width...]
    reduce_scatter x2 -> x0, waiting for transfers between devices: 98.5 us -> none  [the longest x1 49.5 us: local(): lax.psum_scatter(passage_back, 'mp', scatter_dimension=1, tiled=True)]
    unnamed x5 -> x1, waiting for transfers between devices: 67 us -> 0.02 us
    dot_general x4 -> x0, matrix products: 38.9 us -> none  [the longest x1 11.4 us: local(): lax.dot_general(passage_hidden, d_passage_embed, contract, preferred_elem...]
    unnamed x38 -> x44, local copies, waits for them, and re-layouts: 30.2 us -> 22.8 us
  transfers between devices with their start and end apart: 7 -> 4, of which waited for: 6 -> 3; matrix products, arithmetic and copies ran while one was open for 5% -> 1% of each run, Pallas kernels for 0% -> 0%
where the time goes in v2:
time: 459 us; the launch traced here: 452 us
  Pallas kernels  107 us (23%)
  waiting for transfers between devices  100 us (22%)
  blocking collectives  99.1 us (22%)
  local copies, waits for them, and re-layouts  64.9 us (14%)
  matrix products  24.4 us (5%)
  starting transfers between devices  22.6 us (5%)
  other arithmetic  18.4 us (4%)
  between operations  15.2 us (3%)
    all_to_all x1, blocking collectives, local(): lax.all_to_all(outgoing, 'dp', split_axis=0, concat_axis=0, tiled=True)  60.5 us
    pallas_call x1, Pallas kernels, tail(): pl.pallas_call(tail_kernel, out_shape=(jax.ShapeDtypeStruct((share, width...  55.2 us
    pallas_call x1, Pallas kernels, hidden_grad(): pl.pallas_call(hidden_kernel, out_shape=jax.ShapeDtypeStruct((rows, width...  51.8 us
    all_to_all x1, waiting for transfers between devices, local(): lax.all_to_all(reply, 'dp', split_axis=0, concat_axis=0, tiled=True)  50 us
    psum x1, waiting for transfers between devices, local(): lax.psum(similarity_parts.astype(jnp.bfloat16), 'mp').astype(jnp.float32)  39.4 us
    unnamed x44, local copies, waits for them, and re-layouts  22.8 us
    unnamed x1, blocking collectives  20.6 us
    convert_element_type x2, local copies, waits for them, and re-layouts, local(): d_cand[:, block_rows:].reshape(request_count, block_rows, embed_width)  10.8 us
  transfers between devices with their start and end apart: 4, of which 3 were waited for; matrix products, arithmetic and copies ran while one was open for 1% of the time, Pallas kernels for 0%

profile of v2, /device:TPU:1, one launch (start us, length us, event | category | flops | bytes accessed | tf_op | source)
XLA Modules:
  0.0 451.7 jit_solution(17131054925665645208)
XLA Ops:
  7.2 8.4 %multiply_reduce_fusion.1 = (f32[512]{0:T(512)S(1)}, f32[512,1024]{1,0:T(8,128)S(1)}) fusion(bf16[512,4096]{1,0:T(8,128)(2,1)} %query_hbm.1, bf16[4096,1024]{1,0:T(8,128)(2,1)} %head_hbm.3), kind=kOutput, calls=%fused_computation.18 | convolution fusion | flops 4296015360 | bytes 14682112 | tf_op jit(solution)/shard_map/dot_general | solution.py:412
  15.7 5.8 %multiply_reduce_fusion = (f32[512]{0:T(512)S(1)}, f32[512,1024]{1,0:T(8,128)}) fusion(bf16[512,4096]{1,0:T(8,128)(2,1)S(1)} %copy-done.13, bf16[4096,1024]{1,0:T(8,128)(2,1)S(1)} %copy-done), kind=kOutput, calls=%fused_computation.17 | convolution fusion | flops 4296015360 | bytes 14682112 | tf_op jit(solution)/shard_map/dot_general | solution.py:413
  21.5 10.5 %all-reduce.2 = (f32[512]{0:T(512)S(1)}, f32[512]{0:T(512)S(1)}) all-reduce(f32[512]{0:T(512)S(1)} %get-tuple-element.14, f32[512]{0:T(512)S(1)} %get-tuple-element.16), channel_id=1, replica_groups=mesh['dp'=32,'mp'=4] {'mp'}, use_global_device_ids=true, to_apply=%region_1.0 | all-reduce | flops 1024 | bytes 8192 | tf_op jit(solution)/shard_map/psum | solution.py:414
  32.0 1.8 multiply_convert_fusion
  33.8 1.6 reshape_reshape.6
  35.4 2.4 copy.16
  37.8 9.8 %all-to-all-start = ((bf16[32,4,16,256]{3,2,1,0:T(8,128)(2,1)}), bf16[32,4,16,256]{3,2,1,0:T(8,128)(2,1)S(1)}, u32[]{:S(2)}, u32[]{:S(2)}) async-start(bf16[32,4,16,256]{3,2,1,0:T(8,128)(2,1)} %bitcast.69), calls=%async_computation | async-start | bytes 2097152 | tf_op jit(solution)/shard_map/all_to_all | solution.py:430
  47.7 0.6 dynamic-slice
  49.2 20.6 %all-reduce = s32[512]{0:T(512)S(1)} all-reduce(s32[512]{0:T(512)S(1)} %dynamic-update-slice), channel_id=1, replica_groups=mesh['dp'=32,'mp'=4] {'dp'}, use_global_device_ids=true, to_apply=%add | all-reduce | flops 512 | bytes 4096
  69.9 3.4 gather_fusion
  73.4 3.9 broadcast_select_fusion
  77.3 8.3 %all-to-all-start.1 = ((bf16[32,16,16,256]{3,2,1,0:T(8,128)(2,1)}), bf16[32,16,16,256]{3,2,1,0:T(8,128)(2,1)}, u32[]{:S(2)}, u32[]{:S(2)}) async-start(bf16[32,16,16,256]{3,2,1,0:T(8,128)(2,1)} %broadcast_select_fusion), calls=%async_computation.1 | async-start | bytes 8388608 | tf_op jit(solution)/shard_map/all_to_all | solution.py:435
  85.6 0.5 all-reduce.5.cloned.1.call-start
  86.3 50.0 %all-to-all-done.1 = bf16[32,16,16,256]{3,2,1,0:T(8,128)(2,1)} async-done(((bf16[32,16,16,256]{3,2,1,0:T(8,128)(2,1)}), bf16[32,16,16,256]{3,2,1,0:T(8,128)(2,1)}, u32[]{:S(2)}, u32[]{:S(2)}) %all-to-all-start.1) | async-done | bytes 4194336 | tf_op jit(solution)/shard_map/all_to_all | solution.py:435
  136.3 9.5 %copy.17 = bf16[16,8,16,4,256]{4,3,2,1,0:T(4,128)(2,1)} copy(bf16[16,8,16,4,256]{4,2,0,3,1:T(8,128)(2,1)} %bitcast.9) | data formatting | bytes 8388608 | tf_op jit(solution)/shard_map/transpose | solution.py:395
  145.9 7.7 %reshape_reshape.7 = bf16[4,4,128,1024]{3,2,1,0:T(8,128)(2,1)} reshape(bf16[16,8,16,4,256]{4,3,2,1,0:T(4,128)(2,1)} %copy.17) | data formatting | bytes 8388608 | tf_op jit(solution)/shard_map/reshape;reshape | solution.py:436
  153.6 2.9 pad_maximum_fusion
  156.5 2.4 copy-done.5
  158.9 2.7 convolution_convert_fusion.1
  161.5 39.4 %all-reduce.5.cloned.1.call-done = bf16[4,128,640]{2,1,0:T(8,128)(2,1)} async-done(((bf16[4,128,640]{2,1,0:T(8,128)(2,1)}), bf16[4,128,640]{2,1,0:T(8,128)(2,1)}) %all-reduce.5.cloned.1.call-update) | async-done | bytes 655376 | tf_op jit(solution)/shard_map/psum | solution.py:447
  200.9 1.6 fusion.7
  202.5 2.8 fusion.9
  205.2 4.0 copy-done.4
  209.2 2.6 slice.15
  211.8 7.8 %convert_element_type.52 = bf16[16,8,16,4,256]{4,3,2,1,0:T(4,128)(2,1)} reshape(bf16[4,512,1024]{2,1,0:T(8,128)(2,1)} %slice.15) | data formatting | bytes 8388608 | tf_op jit(solution)/shard_map/convert_element_type | solution.py:468
  219.6 3.0 copy.20
  222.6 60.5 %all_to_all.20 = bf16[32,16,16,256]{3,2,1,0:T(8,128)(2,1)S(1)} all-to-all(bf16[32,16,16,256]{3,2,1,0:T(8,128)(2,1)S(1)} %bitcast.62), channel_id=1, replica_groups=mesh['dp'=32,'mp'=4] {'dp'}, dimensions={0} | all-to-all | bytes 8388608 | tf_op jit(solution)/shard_map/all_to_all | solution.py:471
  283.1 2.2 copy.23
  285.3 0.7 convolution_convert_fusion
  286.1 1.2 copy.24
  287.3 4.0 all-to-all-start.3
  291.3 0.6 subtract_bitcast_fusion
  291.9 4.0 fusion.10
  296.0 1.3 copy-done.11
  297.7 10.7 %all-to-all-done.3 = bf16[32,4,16,256]{3,2,1,0:T(8,128)(2,1)S(1)} async-done(((bf16[32,4,16,256]{3,2,1,0:T(8,128)(2,1)}), bf16[32,4,16,256]{3,2,1,0:T(8,128)(2,1)S(1)}, u32[]{:S(2)}, u32[]{:S(2)}) %all-to-all-start.3) | async-done | bytes 1048608 | tf_op jit(solution)/shard_map/all_to_all | solution.py:481
  308.7 1.8 copy.21
  310.5 2.1 reshape.83
  312.6 2.8 slice_add_fusion
  315.4 1.3 copy-done.9
  317.2 7.4 %all-reduce.1 = (f32[512]{0:T(512)S(1)}, f32[512]{0:T(512)S(1)}) all-reduce(f32[512]{0:T(512)S(1)} %fusion.3, f32[512]{0:T(512)S(1)} %fusion), channel_id=1, replica_groups=mesh['dp'=32,'mp'=4] {'mp'}, use_global_device_ids=true, to_apply=%region_8.9 | all-reduce | flops 1024 | bytes 8192 | tf_op jit(solution)/shard_map/psum | solution.py:484
  324.6 3.1 fusion.2.d_passage
  328.1 3.4 copy-done.1
  331.5 51.8 %hidden_grad.1 = bf16[512,1024]{1,0:T(8,128)(2,1)S(1)} custom-call(bf16[512,1024]{1,0:T(8,128)(2,1)S(1)} %fusion.5.d_query.grad, bf16[4096,1024]{1,0:T(8,128)(2,1)S(1)} %copy-done.1), custom_call_target="tpu_custom_call" | custom-call | tf_op jit(solution)/shard_map/hidden_grad/pallas_call | solution.py:104
  383.3 1.0 copy-done.3
  384.2 55.2 %tail.1 = (f32[128,1024]{1,0:T(8,128)}, bf16[512,1024]{1,0:T(8,128)(2,1)}) custom-call(bf16[512,1024]{1,0:T(8,128)(2,1)} %copy-done.2, bf16[512,1024]{1,0:T(8,128)(2,1)} %fusion.2.d_passage, bf16[512,4096]{1,0:T(8,128)(2,1)} %query_hbm.1, bf16[512,4096]{1,0:T(8,128)(2,1)} %passage_hbm.1, bf16[4096,1024]{1,0:T(8,128)(2,1)} %head_hbm.3), custom_call_target="tpu_custom_call" | custom-call | tf_op jit(solution)/shard_map/tail/pallas_call | solution.py:344
  439.4 2.0 copy.30
  441.4 2.3 copy.31
  443.7 1.0 copy.32
  (45 shorter events, 2.3 us)
Async XLA Ops:
  7.2 8.5 %copy-start = (bf16[4096,1024]{1,0:T(8,128)(2,1)S(1)}, bf16[4096,1024]{1,0:T(8,128)(2,1)}, u32[]{:S(2)}) copy-start(bf16[4096,1024]{1,0:T(8,128)(2,1)} %head_hbm.3) | copy-start | bytes 25165828
  7.2 8.5 %copy-start.13 = (bf16[512,4096]{1,0:T(8,128)(2,1)S(1)}, bf16[512,4096]{1,0:T(8,128)(2,1)}, u32[]{:S(2)}) copy-start(bf16[512,4096]{1,0:T(8,128)(2,1)} %passage_hbm.1) | copy-start | bytes 12582916
  15.7 280.3 %copy-start.6 = (f32[512,1024]{1,0:T(8,128)}, f32[512,1024]{1,0:T(8,128)S(1)}, u32[]{:S(2)}) copy-start(f32[512,1024]{1,0:T(8,128)S(1)} %get-tuple-element.15) | copy-start | bytes 6291460
  33.8 4.0 copy-start.10
  35.4 12.2 %copy-start.16 = (s32[4,4]{1,0:T(4,128)S(1)}, s32[4,4]{1,0:T(4,128)}, u32[]{:S(2)}) copy-start(s32[4,4]{1,0:T(4,128)} %param.8) | copy-start | bytes 196
  35.4 12.3 %copy-start.17 = (u32[128]{0:T(128)S(1)}, u32[128]{0:T(128)}, u32[]{:S(2)}) copy-start(u32[128]{0:T(128)} %constant.28) | copy-start | bytes 1540
  37.8 32.1 %all-to-all-start = ((bf16[32,4,16,256]{3,2,1,0:T(8,128)(2,1)}), bf16[32,4,16,256]{3,2,1,0:T(8,128)(2,1)S(1)}, u32[]{:S(2)}, u32[]{:S(2)}) async-start(bf16[32,4,16,256]{3,2,1,0:T(8,128)(2,1)} %bitcast.69), calls=%async_computation | async-start | bytes 2097152 | tf_op jit(solution)/shard_map/all_to_all | solution.py:430
  77.3 59.0 %all-to-all-start.1 = ((bf16[32,16,16,256]{3,2,1,0:T(8,128)(2,1)}), bf16[32,16,16,256]{3,2,1,0:T(8,128)(2,1)}, u32[]{:S(2)}, u32[]{:S(2)}) async-start(bf16[32,16,16,256]{3,2,1,0:T(8,128)(2,1)} %broadcast_select_fusion), calls=%async_computation.1 | async-start | bytes 8388608 | tf_op jit(solution)/shard_map/all_to_all | solution.py:435
  85.6 115.3 %all-reduce.5.cloned.1.call-start = ((), (), s32[]{:S(2)}) async-start(), calls=%async_computation.4 | async-start | bytes 1310720 | tf_op jit(solution)/shard_map/psum | solution.py:447
  156.5 2.4 copy-start.5
  158.9 42.0 %copy-start.15 = (s32[512]{0:T(512)S(1)}, s32[512]{0:T(512)}, u32[]{:S(2)}) copy-start(s32[512]{0:T(512)} %param.9) | copy-start | bytes 6148
  205.2 4.0 copy-start.4
  287.3 21.2 %all-to-all-start.3 = ((bf16[32,4,16,256]{3,2,1,0:T(8,128)(2,1)}), bf16[32,4,16,256]{3,2,1,0:T(8,128)(2,1)S(1)}, u32[]{:S(2)}, u32[]{:S(2)}) async-start(bf16[32,4,16,256]{3,2,1,0:T(8,128)(2,1)} %bitcast.70), calls=%async_computation.3 | async-start | bytes 2097152 | tf_op jit(solution)/shard_map/all_to_all | solution.py:481
  295.9 1.3 copy-start.11
  312.6 4.1 copy-start.8
  315.4 1.3 copy-start.9
  324.6 3.1 copy-start.7
  324.6 3.1 copy-start.12
  328.1 3.4 copy-start.1
  331.5 51.8 %copy-start.2 = (bf16[512,1024]{1,0:T(8,128)(2,1)}, bf16[512,1024]{1,0:T(8,128)(2,1)S(1)}, u32[]{:S(2)}) copy-start(bf16[512,1024]{1,0:T(8,128)(2,1)S(1)} %fusion.5.d_query.grad) | copy-start | bytes 3145732
  383.2 1.0 copy-start.3
  439.4 4.2 copy-start.14
Sparse Core Ops, SparseCore 0:
  161.7 39.1 all-reduce.4

commit v3 on v2

--- a/solution.py
+++ b/solution.py
@@ -379,6 +379,347 @@
     )(d_query, d_passage, query_hidden, passage_hidden, head_weight)
 
 
+OFFSETS = tuple(
+    (dy, dx, core)
+    for dy, dx in (
+        (2, 2), (1, 3), (3, 1), (1, 1), (3, 3), (0, 2), (2, 0), (1, 2),
+        (3, 2), (2, 1), (2, 3), (0, 1), (1, 0), (0, 3), (3, 0), (0, 0),
+    )
+    for core in range(2)
+    if dy or dx or core
+)
+
+
+def plane_peer(offset):
+    y, x, core = place()
+    return (
+        lax.rem(y + offset[0], 4) * 8 + lax.rem(x + offset[1], 4) * 2 + lax.rem(core + offset[2], 2)
+    )
+
+
+def share_rows(device):
+    return pl.ds(pl.multiple_of(lax.div(device, 4) * 16, 16), 16)
+
+
+def share_cols(device):
+    return pl.ds(pl.multiple_of(lax.rem(device, 4) * 256, 256), 256)
+
+
+def diagonal():
+    rows = lax.broadcasted_iota(jnp.int32, (128, 128), 0)
+    return rows == lax.broadcasted_iota(jnp.int32, (128, 128), 1)
+
+
+def as_row(column):
+    spread = jnp.broadcast_to(column, (128, 128))
+    return jnp.sum(jnp.where(diagonal(), spread, 0.0), axis=0, keepdims=True)
+
+
+def as_column(row):
+    spread = jnp.broadcast_to(row, (128, 128))
+    return jnp.sum(jnp.where(diagonal(), spread, 0.0), axis=1, keepdims=True)
+
+
+def depth_copy(src, dst, send_sem, recv_sem, k):
+    return remote(src, dst.at[k - 1], send_sem.at[k - 1], recv_sem.at[k - 1], depth_partner(k))
+
+
+def depth_start(src, dst, send_sem, recv_sem):
+    for k in (2, 1, 3):
+        depth_copy(src, dst, send_sem, recv_sem, k).start()
+
+
+def depth_total(src, dst, send_sem, recv_sem):
+    for k in (1, 3, 2):
+        depth_copy(src, dst, send_sem, recv_sem, k).wait_recv()
+    return src[...] + dst[0] + dst[1] + dst[2]
+
+
+def depth_finish(src, dst, send_sem, recv_sem):
+    for k in (1, 2, 3):
+        depth_copy(src, dst, send_sem, recv_sem, k).wait_send()
+
+
+def front_kernel(
+    query_hbm,
+    passage_hbm,
+    head_hbm,
+    wanted,
+    positions,
+    weights,
+    losses,
+    query_norm,
+    passage_norm,
+    inverses,
+    fetched,
+    all_wanted,
+    head,
+    hidden,
+    embed,
+    held,
+    reply,
+    partial,
+    partial_in,
+    squares,
+    squares_in,
+    table,
+    load_sem,
+    table_sem,
+    square_send,
+    square_recv,
+    want_send,
+    want_recv,
+    spread_send,
+    spread_recv,
+    reply_send,
+    reply_recv,
+    partial_send,
+    partial_recv,
+    weight_send,
+    weight_recv,
+    loss_send,
+    loss_recv,
+):
+    dp = lax.axis_index("dp")
+    mp = lax.axis_index("mp")
+    depth = head.shape[1]
+    hidden_hbm = (passage_hbm, query_hbm)
+
+    def hidden_load(side, chunk):
+        columns = pl.ds(pl.multiple_of(chunk * depth, depth), depth)
+        return pltpu.make_async_copy(
+            hidden_hbm[side].at[:, columns], hidden.at[side, chunk], load_sem.at[side, chunk]
+        )
+
+    def head_chunk(chunk):
+        rows = pl.ds(pl.multiple_of(chunk * depth, depth), depth)
+        return pltpu.make_async_copy(head_hbm.at[rows], head.at[chunk], load_sem.at[2, chunk])
+
+    for chunk in range(4):
+        hidden_load(0, chunk).start()
+        head_chunk(chunk).start()
+    for chunk in range(4):
+        hidden_load(1, chunk).start()
+    embed[...] = jnp.zeros_like(embed)
+    greet(
+        [{"dp": plane_peer(offset)} for offset in OFFSETS]
+        + [depth_partner(k) for k in (1, 2, 3)]
+    )
+
+    def want_copy(j):
+        return remote(
+            wanted,
+            all_wanted.at[dp],
+            want_send.at[j],
+            want_recv.at[j],
+            {"dp": plane_peer(OFFSETS[j])},
+        )
+
+    for j in range(31):
+        want_copy(j).start()
+    all_wanted[dp] = wanted[...]
+
+    def project(side):
+        @pl.loop(0, 4)
+        def _(chunk):
+            hidden_load(side, chunk).wait()
+            if side == 0:
+                head_chunk(chunk).wait()
+
+            @pl.loop(0, 2)
+            def _(i):
+                rows = pl.ds(pl.multiple_of(i * 256, 256), 256)
+                embed[side, rows] += jnp.dot(
+                    hidden[side, chunk, rows], head[chunk], preferred_element_type=jnp.float32
+                )
+
+        for b in range(4):
+            block = embed[side, b * 128 : (b + 1) * 128]
+            squares[side, b : b + 1] = as_row(jnp.sum(block * block, axis=1, keepdims=True))
+        squares[side, 4:8] = jnp.zeros((4, 128), jnp.float32)
+
+    def square_args(side):
+        return squares.at[side], squares_in.at[side], square_send.at[side], square_recv.at[side]
+
+    def normalize(side, out):
+        inverses[side] = lax.rsqrt(depth_total(*square_args(side)) + epsilon)
+        for b in range(4):
+            inverse = as_column(inverses[side, b : b + 1])
+            out[b] = (embed[side, b * 128 : (b + 1) * 128] * inverse).astype(jnp.bfloat16)
+
+    project(0)
+    depth_start(*square_args(0))
+    normalize(0, passage_norm)
+
+    def spread_copy(j):
+        peer = plane_peer(OFFSETS[j])
+        return remote(
+            passage_norm.at[:, share_rows(peer), share_cols(peer)],
+            held.at[pl.ds(dp * 4, 4)],
+            spread_send.at[j],
+            spread_recv.at[j],
+            {"dp": peer},
+        )
+
+    for j in range(31):
+        spread_copy(j).start()
+    for b in range(4):
+        held[dp * 4 + b] = passage_norm[b, share_rows(dp), share_cols(dp)]
+    project(1)
+    depth_start(*square_args(1))
+    normalize(1, query_norm)
+    for j in range(31):
+        want_copy(j).wait_recv()
+    table_copy = pltpu.make_async_copy(all_wanted, table, table_sem)
+    table_copy.start()
+    table_copy.wait()
+    for j in range(31):
+        spread_copy(j).wait_recv()
+
+    def reply_copy(j):
+        peer = plane_peer(OFFSETS[j])
+        return remote(
+            reply.at[peer],
+            fetched.at[:, share_rows(dp), share_cols(dp)],
+            reply_send.at[j],
+            reply_recv.at[j],
+            {"dp": peer},
+        )
+
+    def gather(device):
+        @pl.loop(0, 16, unroll=4)
+        def _(i):
+            reply[device, i] = held[table[device, i, 0]]
+
+    for j in range(31):
+        gather(plane_peer(OFFSETS[j]))
+        reply_copy(j).start()
+    gather(dp)
+    fetched[:, share_rows(dp), share_cols(dp)] = reply[dp]
+    for j in range(31):
+        reply_copy(j).wait_recv()
+
+    def partial_copy(k):
+        return depth_copy(
+            partial.at[lax.rem(mp + k, 4)], partial_in, partial_send, partial_recv, k
+        )
+
+    for k in DEPTH_ORDER:
+        b = lax.rem(mp + k, 4)
+        rows = query_norm[b]
+        partial[b, :, :128] = lax.dot_general(
+            rows, passage_norm[b], COL_CONTRACT, preferred_element_type=jnp.float32
+        ).astype(jnp.bfloat16)
+        others = fetched[pl.ds(b * 4, 4)].reshape(512, depth)
+        partial[b, :, 128:] = lax.dot_general(
+            rows, others, COL_CONTRACT, preferred_element_type=jnp.float32
+        ).astype(jnp.bfloat16)
+        if k:
+            partial_copy(k).start()
+    scores = partial[mp].astype(jnp.float32)
+    for k in (1, 3, 2):
+        partial_copy(k).wait_recv()
+        scores = scores + partial_in[k - 1].astype(jnp.float32)
+    scores = scores / logit_divisor
+    columns = lax.broadcasted_iota(jnp.int32, scores.shape, 1).astype(jnp.float32)
+    matching = (columns == as_column(positions[pl.ds(mp, 1)])).astype(jnp.float32)
+    powers = jnp.exp(scores)
+    totals = jnp.sum(powers, axis=1, keepdims=True)
+    loss = jnp.log(totals) - jnp.sum(scores * matching, axis=1, keepdims=True)
+    weights[mp] = ((powers / totals - matching) / logit_divisor).astype(jnp.bfloat16)
+    losses[mp] = jnp.broadcast_to(as_row(loss), (8, 128))
+
+    def weight_copies(k):
+        return (
+            remote(
+                weights.at[mp],
+                weights.at[mp],
+                weight_send.at[k - 1],
+                weight_recv.at[k - 1],
+                depth_partner(k),
+            ),
+            remote(
+                losses.at[mp],
+                losses.at[mp],
+                loss_send.at[k - 1],
+                loss_recv.at[k - 1],
+                depth_partner(k),
+            ),
+        )
+
+    for k in (2, 1, 3):
+        for copy in weight_copies(k):
+            copy.start()
+    for j in range(31):
+        want_copy(j).wait_send()
+        spread_copy(j).wait_send()
+        reply_copy(j).wait_send()
+    depth_finish(*square_args(0))
+    depth_finish(*square_args(1))
+    for k in (1, 3, 2):
+        partial_copy(k).wait_send()
+        for copy in weight_copies(k):
+            copy.wait()
+
+
+def front(query_hidden, passage_hidden, head_weight, neg_blocks, pos_ids):
+    bf16 = jnp.bfloat16
+    f32 = jnp.float32
+    rows = query_hidden.shape[0]
+    width = head_weight.shape[1]
+    wanted = jnp.broadcast_to(neg_blocks.reshape(16, 1), (16, 128))
+    positions = pos_ids.reshape(4, 128).astype(f32)
+    vmem = pl.BlockSpec(memory_space=pltpu.VMEM)
+    hbm = pl.BlockSpec(memory_space=pl.ANY)
+    dma = pltpu.SemaphoreType.DMA
+    return pl.pallas_call(
+        front_kernel,
+        out_shape=(
+            jax.ShapeDtypeStruct((4, 128, 640), bf16),
+            jax.ShapeDtypeStruct((4, 8, 128), f32),
+            jax.ShapeDtypeStruct((4, 128, width), bf16),
+            jax.ShapeDtypeStruct((4, 128, width), bf16),
+            jax.ShapeDtypeStruct((2, 8, 128), f32),
+            jax.ShapeDtypeStruct((16, 128, width), bf16),
+            jax.ShapeDtypeStruct((32, 16, 128), jnp.int32),
+        ),
+        in_specs=[hbm, hbm, hbm, vmem, vmem],
+        out_specs=(vmem,) * 7,
+        scratch_shapes=[
+            pltpu.VMEM((4, width, width), bf16),
+            pltpu.VMEM((2, 4, rows, width), bf16),
+            pltpu.VMEM((2, rows, width), f32),
+            pltpu.VMEM((128, 16, 256), bf16),
+            pltpu.VMEM((32, 16, 16, 256), bf16),
+            pltpu.VMEM((4, 128, 640), bf16),
+            pltpu.VMEM((3, 128, 640), bf16),
+            pltpu.VMEM((2, 8, 128), f32),
+            pltpu.VMEM((2, 3, 8, 128), f32),
+            pltpu.SMEM((32, 16, 128), jnp.int32),
+            dma((3, 4)),
+            dma,
+            dma((2, 3)),
+            dma((2, 3)),
+            dma((31,)),
+            dma((31,)),
+            dma((31,)),
+            dma((31,)),
+            dma((31,)),
+            dma((31,)),
+            dma((3,)),
+            dma((3,)),
+            dma((3,)),
+            dma((3,)),
+            dma((3,)),
+            dma((3,)),
+        ],
+        compiler_params=pltpu.CompilerParams(
+            collective_id=3, has_side_effects=True, vmem_limit_bytes=VMEM_LIMIT
+        ),
+        name="front",
+    )(query_hidden, passage_hidden, head_weight, wanted, positions)
+
+
 def to_pieces(blocks, row_groups, feature_groups):
     count, rows, cols = blocks.shape
     parts = blocks.reshape(
@@ -408,52 +749,25 @@
     row_groups = dp_count // feature_groups
     piece_rows = block_rows // row_groups
     piece_cols = embed_width // feature_groups
-    all_wanted = lax.all_gather(neg_blocks.reshape(request_count), "dp", tiled=True)
-    query_embed = jnp.dot(query_hidden, head_weight, preferred_element_type=jnp.float32)
-    passage_embed = jnp.dot(passage_hidden, head_weight, preferred_element_type=jnp.float32)
-    query_sq, passage_sq = lax.psum(
-        (
-            jnp.sum(query_embed * query_embed, axis=1),
-            jnp.sum(passage_embed * passage_embed, axis=1),
-        ),
-        "mp",
-    )
-    query_inv = lax.rsqrt(query_sq + epsilon)
-    passage_inv = lax.rsqrt(passage_sq + epsilon)
-    query_unit = query_embed * query_inv[:, None]
-    passage_unit = passage_embed * passage_inv[:, None]
-    query_norm = query_unit.astype(jnp.bfloat16)
-    passage_norm = passage_unit.astype(jnp.bfloat16)
-    query_blocks = query_norm.reshape(block_count, block_rows, embed_width)
-    passage_blocks = passage_norm.reshape(block_count, block_rows, embed_width)
-    pieces = to_pieces(passage_blocks, row_groups, feature_groups)
-    held = lax.all_to_all(pieces, "dp", split_axis=0, concat_axis=0, tiled=True)
-    held = held.reshape(total_blocks, piece_rows, piece_cols)
-    reply = jnp.take(held, all_wanted, axis=0).reshape(
-        dp_count, request_count, piece_rows, piece_cols
-    )
-    arrived = lax.all_to_all(reply, "dp", split_axis=0, concat_axis=0, tiled=True)
-    fetched = from_pieces(arrived, row_groups, feature_groups).reshape(
-        block_count, neg_count, block_rows, embed_width
-    )
-    retrieved_documents = jnp.concatenate([passage_blocks[:, None], fetched], axis=1).reshape(
-        block_count, cand_rows, embed_width
-    )
-    similarity_parts = jnp.einsum(
-        "bqe,bce->bqc", query_blocks, retrieved_documents, preferred_element_type=jnp.float32
-    )
-    positions = pos_ids.reshape(block_count, block_rows)
-    similarity_table = (
-        lax.psum(similarity_parts.astype(jnp.bfloat16), "mp").astype(jnp.float32) / logit_divisor
-    )
-    columns = jnp.arange(cand_rows, dtype=jnp.int32)
-    matching_document_slot = (columns[None, None, :] == positions[:, :, None]).astype(jnp.float32)
-    exponent_values = jnp.exp(similarity_table)
-    normalizer_totals = jnp.sum(exponent_values, axis=2)
-    losses = jnp.log(normalizer_totals) - jnp.sum(similarity_table * matching_document_slot, axis=2)
-    attention_probabilities = (
-        (exponent_values / normalizer_totals[:, :, None] - matching_document_slot) / logit_divisor
-    ).astype(jnp.bfloat16)
+    (
+        attention_probabilities,
+        losses,
+        query_blocks,
+        passage_blocks,
+        inverses,
+        fetched,
+        wanted_table,
+    ) = front(query_hidden, passage_hidden, head_weight, neg_blocks, pos_ids)
+    all_wanted = wanted_table[:, :, 0].reshape(dp_count * request_count)
+    losses = losses[:, 0]
+    passage_inv = inverses[0, :4].reshape(row_count)
+    query_inv = inverses[1, :4].reshape(row_count)
+    query_unit = query_blocks.reshape(row_count, embed_width).astype(jnp.float32)
+    passage_unit = passage_blocks.reshape(row_count, embed_width).astype(jnp.float32)
+    retrieved_documents = jnp.concatenate(
+        [passage_blocks[:, None], fetched.reshape(block_count, neg_count, block_rows, embed_width)],
+        axis=1,
+    ).reshape(block_count, cand_rows, embed_width)
     d_query = jnp.einsum(
         "bqc,bce->bqe",
         attention_probabilities,

time: 459 us -> 360 us (0.78); the launches traced: 452 us -> 360 us
  Pallas kernels: 107 us -> 215 us
  blocking collectives: 99.1 us -> 6.78 us
  waiting for transfers between devices: 100 us -> 60.6 us
  local copies, waits for them, and re-layouts: 64.9 us -> 43.5 us
  matrix products: 24.4 us -> 6.1 us
  between operations: 15.2 us -> 0.8 us
  starting transfers between devices: 22.6 us -> 15 us
  other arithmetic: 18.4 us -> 12 us
    pallas_call x0 -> x1, Pallas kernels: none -> 108 us  [front(): pl.pallas_call(front_kernel, out_shape=(jax.ShapeDtypeStruct((4, 128, 640...]
    all_to_all x1 -> x0, blocking collectives: 60.5 us -> none  [local(): lax.all_to_all(outgoing, 'dp', split_axis=0, concat_axis=0, tiled=True)]
    psum x1 -> x0, waiting for transfers between devices: 39.4 us -> none  [local(): lax.psum(similarity_parts.astype(jnp.bfloat16), 'mp').astype(jnp.float32)]
    unnamed x1 -> x0, blocking collectives: 20.6 us -> none
    dot_general x3 -> x0, matrix products: 16.9 us -> none  [the longest x1 8.45 us: local(): jnp.dot(query_hidden, head_weight, preferred_element_type=jnp.float32)]
    another operation x3 -> x0, local copies, waits for them, and re-layouts: 11.7 us -> none  [the longest x1 7.7 us: local(): from_pieces(arrived, row_groups, feature_groups)]
    psum x1 -> x0, blocking collectives: 10.5 us -> none  [local(): lax.psum((jnp.sum(query_embed * query_embed, axis=1), jnp.sum(passage_emb...]
    all_to_all x2 -> x1, starting transfers between devices: 18.1 us -> 7.83 us  [local(): lax.all_to_all(outgoing, 'dp', split_axis=0, concat_axis=0, tiled=True)]
  transfers between devices with their start and end apart: 4 -> 2, of which waited for: 3 -> 2; matrix products, arithmetic and copies ran while one was open for 1% -> 2% of each run, Pallas kernels for 0% -> 0%
where the time goes in v3:
time: 360 us
  Pallas kernels  215 us (60%)
  waiting for transfers between devices  60.6 us (17%)
  local copies, waits for them, and re-layouts  43.5 us (12%)
  starting transfers between devices  15 us (4%)
  other arithmetic  12 us (3%)
  blocking collectives  6.78 us (2%)
  matrix products  6.1 us (2%)
    pallas_call x1, Pallas kernels, front(): pl.pallas_call(front_kernel, out_shape=(jax.ShapeDtypeStruct((4, 128, 640...  108 us
    pallas_call x1, Pallas kernels, tail(): pl.pallas_call(tail_kernel, out_shape=(jax.ShapeDtypeStruct((share, width...  55.3 us
    pallas_call x1, Pallas kernels, hidden_grad(): pl.pallas_call(hidden_kernel, out_shape=jax.ShapeDtypeStruct((rows, width...  51.8 us
    all_to_all x1, waiting for transfers between devices, local(): lax.all_to_all(outgoing, 'dp', split_axis=0, concat_axis=0, tiled=True)  50 us
    unnamed x27, local copies, waits for them, and re-layouts  18.3 us
    convert_element_type x2, local copies, waits for them, and re-layouts, local(): d_cand[:, block_rows:].reshape(request_count, block_rows, embed_width)  12.8 us
    all_to_all x1, waiting for transfers between devices, local(): home = lax.all_to_all(summed, 'dp', split_axis=0, concat_axis=0, tiled=True)  10.7 us
    all_to_all x1, starting transfers between devices, local(): lax.all_to_all(outgoing, 'dp', split_axis=0, concat_axis=0, tiled=True)  7.83 us
  transfers between devices with their start and end apart: 2, of which 2 were waited for; matrix products, arithmetic and copies ran while one was open for 2% of the time, Pallas kernels for 0%

profile of v3, /device:TPU:1, one launch (start us, length us, event | category | flops | bytes accessed | tf_op | source)
XLA Modules:
  0.0 359.6 jit_solution(4230905830046584544)
XLA Ops:
  0.6 0.8 broadcast_in_dim.6
  1.4 1.3 convert_bitcast_fusion.1.positions
  2.7 0.7 broadcast_in_dim.14.wanted
  3.3 107.7 %front.1 = (bf16[4,128,640]{2,1,0:T(8,128)(2,1)}, f32[4,8,128]{2,1,0:T(8,128)}, bf16[4,128,1024]{2,1,0:T(8,128)(2,1)}, bf16[4,128,1024]{2,1,0:T(8,128)(2,1)}, f3...) custom-call(bf16[512,4096]{1,0:T(8,128)(2,1)} %query_hbm.3, ...), custom_call_target="tpu_custom_call" | custom-call | tf_op jit(solution)/shard_map/front/pallas_call | solution.py:675
  111.0 3.0 fusion.7
  114.0 0.0 copy-start.4
  114.0 4.0 %copy-done.4 = f32[4,640,1024]{2,1,0:T(8,128)} copy-done((f32[4,640,1024]{2,1,0:T(8,128)}, f32[4,640,1024]{2,1,0:T(8,128)S(1)}, u32[]{:S(2)}) %copy-start.4) | copy-done | bytes 10485784
  118.0 2.6 slice.32
  120.6 7.8 %convert_element_type.56 = bf16[16,8,16,4,256]{4,3,2,1,0:T(4,128)(2,1)} reshape(bf16[4,512,1024]{2,1,0:T(8,128)(2,1)} %slice.32) | data formatting | bytes 8388608 | tf_op jit(solution)/shard_map/convert_element_type | solution.py:782
  128.5 4.9 %copy.13 = bf16[16,8,16,4,256]{4,2,0,3,1:T(8,128)(2,1)} copy(bf16[16,8,16,4,256]{4,3,2,1,0:T(4,128)(2,1)} %convert_element_type.56) | data formatting | bytes 8388608 | tf_op jit(solution)/shard_map/convert_element_type | solution.py:782
  133.4 7.8 %all-to-all-start = ((bf16[32,16,16,256]{3,2,1,0:T(8,128)(2,1)}), bf16[32,16,16,256]{3,2,1,0:T(8,128)(2,1)}, u32[]{:S(2)}, u32[]{:S(2)}) async-start(bf16[32,16,16,256]{3,2,1,0:T(8,128)(2,1)} %bitcast.53), calls=%async_computation | async-start | bytes 8388608 | tf_op jit(solution)/shard_map/all_to_all | solution.py:785
  141.2 0.0 copy-done.9
  141.2 0.6 slice_reduce_fusion
  141.9 0.1 eq.15
  141.9 50.0 %all-to-all-done = bf16[32,16,16,256]{3,2,1,0:T(8,128)(2,1)} async-done(((bf16[32,16,16,256]{3,2,1,0:T(8,128)(2,1)}), bf16[32,16,16,256]{3,2,1,0:T(8,128)(2,1)}, u32[]{:S(2)}, u32[]{:S(2)}) %all-to-all-start) | async-done | bytes 4194336 | tf_op jit(solution)/shard_map/all_to_all | solution.py:785
  191.9 4.4 %copy.16 = bf16[64,8,16,256]{3,1,2,0:T(8,128)(2,1)S(1)} copy(bf16[64,8,16,256]{3,2,1,0:T(8,128)(2,1)} %bitcast.22) | data formatting | bytes 8388608
  196.3 0.7 convolution_convert_fusion
  197.1 0.0 copy-start.10
  197.1 0.0 copy-start.6
  197.1 1.2 copy.17
  198.3 7.2 %all-to-all-start.1 = ((bf16[32,4,16,256]{3,2,1,0:T(8,128)(2,1)}), bf16[32,4,16,256]{3,2,1,0:T(8,128)(2,1)S(1)}, u32[]{:S(2)}, u32[]{:S(2)}) async-start(bf16[32,4,16,256]{3,2,1,0:T(8,128)(2,1)} %bitcast.26), calls=%async_computation.1 | async-start | bytes 2097152 | tf_op jit(solution)/shard_map/all_to_all | solution.py:795
  205.5 1.3 slice.19
  206.8 0.0 copy-done.10
  206.8 0.0 copy-done.6
  206.8 0.0 copy-start.7
  206.8 2.8 pad_maximum_fusion
  209.6 0.0 copy-done.5
  209.6 0.0 copy-done.7
  209.6 2.4 multiply_reduce_fusion.1
  212.0 10.7 %all-to-all-done.1 = bf16[32,4,16,256]{3,2,1,0:T(8,128)(2,1)S(1)} async-done(((bf16[32,4,16,256]{3,2,1,0:T(8,128)(2,1)}), bf16[32,4,16,256]{3,2,1,0:T(8,128)(2,1)S(1)}, u32[]{:S(2)}, u32[]{:S(2)}) %all-to-all-start.1) | async-done | bytes 1048608 | tf_op jit(solution)/shard_map/all_to_all | solution.py:795
  222.7 0.3 convert_bitcast_fusion
  222.9 3.1 copy.14
  226.0 3.3 reshape.64
  229.3 3.8 %multiply_reduce_fusion = (f32[4,128]{1,0:T(4,128)S(1)}, f32[4,128,1024]{2,1,0:T(8,128)}) fusion(bf16[4,128,1024]{2,1,0:T(8,128)(2,1)S(1)} %copy-done.6, f32[4,128,1024]{2,1,0:T(8,128)} %reshape.64, f32[4,640,1024]{2,1,0:T(8,128)} %copy-done.4), kind=kLoop, calls=%fused_computation.13 | loop fusion | flops 2096640 | bytes 7342080 | tf_op jit(solution)/shard_map/reduce_sum | solution.py:799
  233.1 6.8 %all-reduce = (f32[512]{0:T(512)S(1)}, f32[512]{0:T(512)S(1)}) all-reduce(f32[512]{0:T(512)S(1)} %bitcast.59, f32[512]{0:T(512)S(1)} %bitcast.60), channel_id=1, replica_groups=mesh['dp'=32,'mp'=4] {'mp'}, use_global_device_ids=true, to_apply=%region_1.0 | all-reduce | flops 1024 | bytes 8192 | tf_op jit(solution)/shard_map/psum | solution.py:798
  239.9 3.9 %fusion.2 = (bf16[512,1024]{1,0:T(8,128)(2,1)}, bf16[512,1024]{1,0:T(8,128)(2,1)S(1)}) fusion(f32[4,128,1024]{2,1,0:T(8,128)} %get-tuple-element.25, f32[512]{0:T(512)S(1)} %get-tuple-element.23, f32[512]{0:T(512)S(1)} %get-tuple-element.26, bf16[4,128,1024]{2,1,0:T(8,128)(2,1)S(1)} %copy-done.6, f32[512]{0:T(512)S(1)} %get-tuple-element.22, ...), kind=kLoop, calls=%fused_computation.8 | loop fusion | flops 5242880 | bytes 8396800 | tf_op jit(solution)/shard_map/convert_element_type | solution.py:13
  243.8 3.8 %copy-done = bf16[4096,1024]{1,0:T(8,128)(2,1)S(1)} copy-done((bf16[4096,1024]{1,0:T(8,128)(2,1)S(1)}, bf16[4096,1024]{1,0:T(8,128)(2,1)}, u32[]{:S(2)}) %copy-start) | copy-done | bytes 8388632
  247.5 51.8 %hidden_grad.1 = bf16[512,1024]{1,0:T(8,128)(2,1)S(1)} custom-call(bf16[512,1024]{1,0:T(8,128)(2,1)S(1)} %get-tuple-element.31.d_query.grad, bf16[4096,1024]{1,0:T(8,128)(2,1)S(1)} %copy-done), custom_call_target="tpu_custom_call" | custom-call | tf_op jit(solution)/shard_map/hidden_grad/pallas_call | solution.py:104
  299.3 0.0 copy-done.1
  299.3 0.0 copy-start.2
  299.3 1.0 copy-done.2
  300.3 55.3 %tail.1 = (f32[128,1024]{1,0:T(8,128)}, bf16[512,1024]{1,0:T(8,128)(2,1)}) custom-call(bf16[512,1024]{1,0:T(8,128)(2,1)} %copy-done.1, bf16[512,1024]{1,0:T(8,128)(2,1)} %get-tuple-element.30.d_passage, bf16[512,4096]{1,0:T(8,128)(2,1)} %query_hbm.3, bf16[512,4096]{1,0:T(8,128)(2,1)} %passage_hbm.3, bf16[4096,1024]{1,0:T(8,128)(2,1)} %head_hbm.5), custom_call_target="tpu_custom_call" | custom-call | tf_op jit(solution)/shard_map/tail/pallas_call | solution.py:344
  355.6 0.0 copy-start.8
  355.6 2.0 copy.21
  357.6 0.0 copy-done.3
  357.6 1.0 copy.22
  358.6 0.0 copy-done.8
  358.6 1.0 copy.23
  (6 shorter events, 0.0 us)
Async XLA Ops:
  114.0 4.0 %copy-start.4 = (f32[4,640,1024]{2,1,0:T(8,128)}, f32[4,640,1024]{2,1,0:T(8,128)S(1)}, u32[]{:S(2)}) copy-start(f32[4,640,1024]{2,1,0:T(8,128)S(1)} %fusion.7) | copy-start | bytes 31457284
  133.4 7.8 %copy-start.9 = (s32[32,16,128]{2,1,0:T(8,128)S(1)}, s32[32,16,128]{2,1,0:T(8,128)}, u32[]{:S(2)}) copy-start(s32[32,16,128]{2,1,0:T(8,128)} %get-tuple-element.19) | copy-start | bytes 786436
  133.4 58.5 %all-to-all-start = ((bf16[32,16,16,256]{3,2,1,0:T(8,128)(2,1)}), bf16[32,16,16,256]{3,2,1,0:T(8,128)(2,1)}, u32[]{:S(2)}, u32[]{:S(2)}) async-start(bf16[32,16,16,256]{3,2,1,0:T(8,128)(2,1)} %bitcast.53), calls=%async_computation | async-start | bytes 8388608 | tf_op jit(solution)/shard_map/all_to_all | solution.py:785
  197.1 9.7 %copy-start.10 = (f32[2,8,128]{2,1,0:T(8,128)S(1)}, f32[2,8,128]{2,1,0:T(8,128)}, u32[]{:S(2)}) copy-start(f32[2,8,128]{2,1,0:T(8,128)} %get-tuple-element.14) | copy-start | bytes 24580
  197.1 9.7 %copy-start.6 = (bf16[4,128,1024]{2,1,0:T(8,128)(2,1)S(1)}, bf16[4,128,1024]{2,1,0:T(8,128)(2,1)}, u32[]{:S(2)}) copy-start(bf16[4,128,1024]{2,1,0:T(8,128)(2,1)} %get-tuple-element.16) | copy-start | bytes 3145732
  198.3 24.3 %all-to-all-start.1 = ((bf16[32,4,16,256]{3,2,1,0:T(8,128)(2,1)}), bf16[32,4,16,256]{3,2,1,0:T(8,128)(2,1)S(1)}, u32[]{:S(2)}, u32[]{:S(2)}) async-start(bf16[32,4,16,256]{3,2,1,0:T(8,128)(2,1)} %bitcast.26), calls=%async_computation.1 | async-start | bytes 2097152 | tf_op jit(solution)/shard_map/all_to_all | solution.py:795
  206.8 2.8 copy-start.5
  206.8 2.8 copy-start.7
  243.8 55.5 %copy-start.1 = (bf16[512,1024]{1,0:T(8,128)(2,1)}, bf16[512,1024]{1,0:T(8,128)(2,1)S(1)}, u32[]{:S(2)}) copy-start(bf16[512,1024]{1,0:T(8,128)(2,1)S(1)} %get-tuple-element.31.d_query.grad) | copy-start | bytes 3145732
  243.8 3.8 %copy-start = (bf16[4096,1024]{1,0:T(8,128)(2,1)S(1)}, bf16[4096,1024]{1,0:T(8,128)(2,1)}, u32[]{:S(2)}) copy-start(bf16[4096,1024]{1,0:T(8,128)(2,1)} %head_hbm.5) | copy-start | bytes 25165828
  299.3 1.0 copy-start.2
  300.3 57.3 %copy-start.3 = (bf16[512,1024]{1,0:T(8,128)(2,1)S(1)}, bf16[512,1024]{1,0:T(8,128)(2,1)}, u32[]{:S(2)}) copy-start(bf16[512,1024]{1,0:T(8,128)(2,1)} %copy-done.2) | copy-start | bytes 3145732
  355.6 3.0 copy-start.8

commit v4 on v3

--- a/solution.py
+++ b/solution.py
@@ -7,10 +7,6 @@
 
 logit_divisor = 0.02
 epsilon = 1e-06
-
-
-def back_norm(inverse, unit_rows, d_unit, inner):
-    return (inverse[:, None] * (d_unit - unit_rows * inner[:, None])).astype(jnp.bfloat16)
 
 
 MESH = pl.DeviceIdType.MESH
@@ -91,36 +87,6 @@
         hidden_send(part, landed, send_sem, recv_sem, k).wait_send()
 
 
-def hidden_kernel(grad, head_hbm, out, head, part, landed, load_sem, send_sem, recv_sem):
-    for k in DEPTH_ORDER:
-        head_load(head_hbm, head, load_sem, k).start()
-    greet([depth_partner(k) for k in (1, 2, 3)])
-    hidden_parts(grad, head_hbm, head, part, landed, load_sem, send_sem, recv_sem)
-    hidden_sum(part, landed, send_sem, recv_sem, out)
-
-
-def hidden_grad(grad, head_weight):
-    rows, width = grad.shape
-    return pl.pallas_call(
-        hidden_kernel,
-        out_shape=jax.ShapeDtypeStruct((rows, width), jnp.bfloat16),
-        in_specs=[pl.BlockSpec(memory_space=pltpu.VMEM), pl.BlockSpec(memory_space=pl.ANY)],
-        out_specs=pl.BlockSpec(memory_space=pltpu.VMEM),
-        scratch_shapes=[
-            pltpu.VMEM((4, width, width), jnp.bfloat16),
-            pltpu.VMEM((4, rows, width), jnp.bfloat16),
-            pltpu.VMEM((3, rows, width), jnp.bfloat16),
-            pltpu.SemaphoreType.DMA((4,)),
-            pltpu.SemaphoreType.DMA((3,)),
-            pltpu.SemaphoreType.DMA((3,)),
-        ],
-        compiler_params=pltpu.CompilerParams(
-            collective_id=1, has_side_effects=True, vmem_limit_bytes=32 * 1024 * 1024
-        ),
-        name="hidden_grad",
-    )(grad, head_weight)
-
-
 def place():
     dp = lax.axis_index("dp")
     return lax.div(dp, 8), lax.rem(lax.div(dp, 2), 4), lax.rem(dp, 2)
@@ -130,14 +96,253 @@
     return {"dp": y * 8 + x * 2 + core}
 
 
+OFFSETS = tuple(
+    (dy, dx, core)
+    for dy, dx in (
+        (2, 2), (1, 3), (3, 1), (1, 1), (3, 3), (0, 2), (2, 0), (1, 2),
+        (3, 2), (2, 1), (2, 3), (0, 1), (1, 0), (0, 3), (3, 0), (0, 0),
+    )
+    for core in range(2)
+    if dy or dx or core
+)
+
+
+def plane_peer(offset):
+    y, x, core = place()
+    return (
+        lax.rem(y + offset[0], 4) * 8 + lax.rem(x + offset[1], 4) * 2 + lax.rem(core + offset[2], 2)
+    )
+
+
+def share_rows(device):
+    return pl.ds(pl.multiple_of(lax.div(device, 4) * 16, 16), 16)
+
+
+def share_cols(device):
+    return pl.ds(pl.multiple_of(lax.rem(device, 4) * 256, 256), 256)
+
+
+def diagonal():
+    rows = lax.broadcasted_iota(jnp.int32, (128, 128), 0)
+    return rows == lax.broadcasted_iota(jnp.int32, (128, 128), 1)
+
+
+def as_row(column):
+    spread = jnp.broadcast_to(column, (128, 128))
+    return jnp.sum(jnp.where(diagonal(), spread, 0.0), axis=0, keepdims=True)
+
+
+def as_column(row):
+    spread = jnp.broadcast_to(row, (128, 128))
+    return jnp.sum(jnp.where(diagonal(), spread, 0.0), axis=1, keepdims=True)
+
+
+def depth_copy(src, dst, send_sem, recv_sem, k):
+    return remote(src, dst.at[k - 1], send_sem.at[k - 1], recv_sem.at[k - 1], depth_partner(k))
+
+
+def depth_start(src, dst, send_sem, recv_sem):
+    for k in (2, 1, 3):
+        depth_copy(src, dst, send_sem, recv_sem, k).start()
+
+
+def depth_total(src, dst, send_sem, recv_sem):
+    for k in (1, 3, 2):
+        depth_copy(src, dst, send_sem, recv_sem, k).wait_recv()
+    return src[...] + dst[0] + dst[1] + dst[2]
+
+
+def depth_finish(src, dst, send_sem, recv_sem):
+    for k in (1, 2, 3):
+        depth_copy(src, dst, send_sem, recv_sem, k).wait_send()
+
+
+def back_kernel(
+    weights,
+    query_norm,
+    passage_norm,
+    fetched,
+    inverses,
+    head_hbm,
+    d_query_embed,
+    own_terms,
+    returned,
+    hidden_out,
+    head,
+    d_query,
+    outgoing,
+    part,
+    landed,
+    inner,
+    inner_in,
+    load_sem,
+    depth_send,
+    depth_recv,
+    return_send,
+    return_recv,
+    inner_send,
+    inner_recv,
+):
+    dp = lax.axis_index("dp")
+    width = head.shape[1]
+    for k in DEPTH_ORDER:
+        head_load(head_hbm, head, load_sem, k).start()
+    greet(
+        [{"dp": plane_peer(offset)} for offset in OFFSETS]
+        + [depth_partner(k) for k in (1, 2, 3)]
+    )
+
+    @pl.loop(0, 4)
+    def _(b):
+        outgoing[pl.ds(b * 4, 4)] = (
+            lax.dot_general(
+                weights[b, :, 128:],
+                query_norm[b],
+                ROW_CONTRACT,
+                preferred_element_type=jnp.float32,
+            )
+            .astype(jnp.bfloat16)
+            .reshape(4, 128, width)
+        )
+
+    def return_copy(j):
+        peer = plane_peer(OFFSETS[j])
+        return remote(
+            outgoing.at[:, share_rows(peer), share_cols(peer)],
+            returned.at[dp],
+            return_send.at[j],
+            return_recv.at[j],
+            {"dp": peer},
+        )
+
+    for j in range(31):
+        return_copy(j).start()
+    returned[dp] = outgoing[:, share_rows(dp), share_cols(dp)]
+    inner[4:8] = jnp.zeros((4, 128), jnp.float32)
+
+    for b in range(4):
+        total = jnp.dot(
+            weights[b, :, :128], passage_norm[b], preferred_element_type=jnp.float32
+        ) + jnp.dot(
+            weights[b, :, 128:],
+            fetched[4 * b : 4 * b + 4].reshape(512, width),
+            preferred_element_type=jnp.float32,
+        )
+        d_query[b] = total
+        inner[b : b + 1] = as_row(
+            jnp.sum(query_norm[b].astype(jnp.float32) * total, axis=1, keepdims=True)
+        )
+    inner_args = (inner, inner_in, inner_send, inner_recv)
+    depth_start(*inner_args)
+
+    @pl.loop(0, 4)
+    def _(b):
+        own_terms[b] = lax.dot_general(
+            weights[b, :, :128], query_norm[b], ROW_CONTRACT, preferred_element_type=jnp.float32
+        )
+
+    total_inner = depth_total(*inner_args)
+    for b in range(4):
+        d_query_embed[b * 128 : (b + 1) * 128] = embed_grad(
+            inverses[1, b : b + 1], query_norm[b], d_query[b], total_inner[b : b + 1]
+        )
+    hidden_parts(d_query_embed, head_hbm, head, part, landed, load_sem, depth_send, depth_recv)
+    hidden_sum(part, landed, depth_send, depth_recv, hidden_out)
+    for j in range(31):
+        return_copy(j).wait_recv()
+    depth_finish(*inner_args)
+    for j in range(31):
+        return_copy(j).wait_send()
+
+
+def embed_grad(inverse_row, unit, d_unit, inner_row):
+    return (
+        as_column(inverse_row) * (d_unit - unit.astype(jnp.float32) * as_column(inner_row))
+    ).astype(jnp.bfloat16)
+
+
+def back(weights, query_norm, passage_norm, fetched, inverses, head_weight):
+    bf16 = jnp.bfloat16
+    f32 = jnp.float32
+    width = head_weight.shape[1]
+    vmem = pl.BlockSpec(memory_space=pltpu.VMEM)
+    dma = pltpu.SemaphoreType.DMA
+    return pl.pallas_call(
+        back_kernel,
+        out_shape=(
+            jax.ShapeDtypeStruct((512, width), bf16),
+            jax.ShapeDtypeStruct((4, 128, width), f32),
+            jax.ShapeDtypeStruct((32, 16, 16, 256), bf16),
+            jax.ShapeDtypeStruct((512, width), bf16),
+        ),
+        in_specs=[vmem] * 5 + [pl.BlockSpec(memory_space=pl.ANY)],
+        out_specs=(vmem,) * 4,
+        scratch_shapes=[
+            pltpu.VMEM((4, width, width), bf16),
+            pltpu.VMEM((4, 128, width), f32),
+            pltpu.VMEM((16, 128, width), bf16),
+            pltpu.VMEM((4, 512, width), bf16),
+            pltpu.VMEM((3, 512, width), bf16),
+            pltpu.VMEM((8, 128), f32),
+            pltpu.VMEM((3, 8, 128), f32),
+            dma((4,)),
+            dma((3,)),
+            dma((3,)),
+            dma((31,)),
+            dma((31,)),
+            dma((3,)),
+            dma((3,)),
+        ],
+        compiler_params=pltpu.CompilerParams(
+            collective_id=1, has_side_effects=True, vmem_limit_bytes=VMEM_LIMIT
+        ),
+        name="back",
+    )(weights, query_norm, passage_norm, fetched, inverses, head_weight)
+
+
+def add_kernel(table, returned, out, total):
+    total[...] = jnp.zeros_like(total)
+
+    @pl.loop(0, 512, unroll=4)
+    def _(i):
+        block = table[i]
+        total[block] += returned[i].astype(jnp.float32)
+
+    out[...] = total[...].astype(jnp.bfloat16)
+
+
+def add_returned(table, returned):
+    vmem = pl.BlockSpec(memory_space=pltpu.VMEM)
+    return pl.pallas_call(
+        add_kernel,
+        out_shape=jax.ShapeDtypeStruct((128, 16, 256), jnp.bfloat16),
+        in_specs=[pl.BlockSpec(memory_space=pltpu.SMEM), vmem],
+        out_specs=vmem,
+        scratch_shapes=[pltpu.VMEM((128, 16, 256), jnp.float32)],
+        name="add_returned",
+    )(table, returned)
+
+
 def tail_kernel(
     d_query,
-    d_passage,
+    block_sums,
+    own_terms,
+    passage_norm,
+    inverses,
     query_hbm,
     passage_hbm,
     head_hbm,
     weight_out,
     hidden_out,
+    home,
+    d_total,
+    d_passage,
+    inner,
+    inner_in,
+    home_send,
+    home_recv,
+    inner_send,
+    inner_recv,
     head,
     query,
     passage,
@@ -184,11 +389,40 @@
     for copy in hidden_loads(0, 0) + hidden_loads(1, 1):
         copy.start()
     greet(
-        [depth_partner(k) for k in (1, 2, 3)]
-        + [at(y, x, 1 - core)]
-        + [at(lax.rem(y + k, 4), x, core) for k in (1, 2, 3)]
-        + [at(y, lax.rem(x + k, 4), core) for k in (1, 2, 3)]
-    )
+        [{"dp": plane_peer(offset)} for offset in OFFSETS]
+        + [depth_partner(k) for k in (1, 2, 3)]
+    )
+    dp = lax.axis_index("dp")
+
+    def home_copy(j):
+        peer = plane_peer(OFFSETS[j])
+        return remote(
+            block_sums.at[pl.ds(peer * 4, 4)],
+            home.at[:, share_rows(dp), share_cols(dp)],
+            home_send.at[j],
+            home_recv.at[j],
+            {"dp": peer},
+        )
+
+    for j in range(31):
+        home_copy(j).start()
+    home[:, share_rows(dp), share_cols(dp)] = block_sums[pl.ds(dp * 4, 4)]
+    inner[4:8] = jnp.zeros((4, 128), jnp.float32)
+    for j in range(31):
+        home_copy(j).wait_recv()
+    for b in range(4):
+        total = own_terms[b] + home[b].astype(jnp.float32)
+        d_total[b] = total
+        inner[b : b + 1] = as_row(
+            jnp.sum(passage_norm[b].astype(jnp.float32) * total, axis=1, keepdims=True)
+        )
+    inner_args = (inner, inner_in, inner_send, inner_recv)
+    depth_start(*inner_args)
+    total_inner = depth_total(*inner_args)
+    for b in range(4):
+        d_passage[b * 128 : (b + 1) * 128] = embed_grad(
+            inverses[0, b : b + 1], passage_norm[b], d_total[b], total_inner[b : b + 1]
+        )
     hidden_parts(d_passage, head_hbm, head, part, landed, load_sem, depth_send, depth_recv)
 
     def core_copy(chip):
@@ -317,6 +551,9 @@
                 jnp.float32
             )
     hidden_sum(part, landed, depth_send, depth_recv, hidden_out)
+    for j in range(31):
+        home_copy(j).wait_send()
+    depth_finish(*inner_args)
 
     @pl.loop(0, 16)
     def _(chip):
@@ -333,7 +570,16 @@
             second_copy(side, k).wait_send()
 
 
-def tail(d_query, d_passage, query_hidden, passage_hidden, head_weight):
+def tail(
+    d_query,
+    block_sums,
+    own_terms,
+    passage_norm,
+    inverses,
+    query_hidden,
+    passage_hidden,
+    head_weight,
+):
     rows, width = d_query.shape
     hidden = head_weight.shape[0]
     share = hidden // 32
@@ -347,9 +593,18 @@
             jax.ShapeDtypeStruct((share, width), jnp.float32),
             jax.ShapeDtypeStruct((rows, width), bf16),
         ),
-        in_specs=[vmem, vmem, hbm, hbm, hbm],
+        in_specs=[vmem] * 5 + [hbm] * 3,
         out_specs=(vmem, vmem),
         scratch_shapes=[
+            pltpu.VMEM((4, 128, width), bf16),
+            pltpu.VMEM((4, 128, width), jnp.float32),
+            pltpu.VMEM((rows, width), bf16),
+            pltpu.VMEM((8, 128), jnp.float32),
+            pltpu.VMEM((3, 8, 128), jnp.float32),
+            dma((31,)),
+            dma((31,)),
+            dma((3,)),
+            dma((3,)),
             pltpu.VMEM((4, width, width), bf16),
             pltpu.VMEM((2, rows, 4 * share), bf16),
             pltpu.VMEM((2, rows, 4 * share), bf16),
@@ -376,68 +631,16 @@
             collective_id=2, has_side_effects=True, vmem_limit_bytes=VMEM_LIMIT
         ),
         name="tail",
-    )(d_query, d_passage, query_hidden, passage_hidden, head_weight)
-
-
-OFFSETS = tuple(
-    (dy, dx, core)
-    for dy, dx in (
-        (2, 2), (1, 3), (3, 1), (1, 1), (3, 3), (0, 2), (2, 0), (1, 2),
-        (3, 2), (2, 1), (2, 3), (0, 1), (1, 0), (0, 3), (3, 0), (0, 0),
-    )
-    for core in range(2)
-    if dy or dx or core
-)
-
-
-def plane_peer(offset):
-    y, x, core = place()
-    return (
-        lax.rem(y + offset[0], 4) * 8 + lax.rem(x + offset[1], 4) * 2 + lax.rem(core + offset[2], 2)
-    )
-
-
-def share_rows(device):
-    return pl.ds(pl.multiple_of(lax.div(device, 4) * 16, 16), 16)
-
-
-def share_cols(device):
-    return pl.ds(pl.multiple_of(lax.rem(device, 4) * 256, 256), 256)
-
-
-def diagonal():
-    rows = lax.broadcasted_iota(jnp.int32, (128, 128), 0)
-    return rows == lax.broadcasted_iota(jnp.int32, (128, 128), 1)
-
-
-def as_row(column):
-    spread = jnp.broadcast_to(column, (128, 128))
-    return jnp.sum(jnp.where(diagonal(), spread, 0.0), axis=0, keepdims=True)
-
-
-def as_column(row):
-    spread = jnp.broadcast_to(row, (128, 128))
-    return jnp.sum(jnp.where(diagonal(), spread, 0.0), axis=1, keepdims=True)
-
-
-def depth_copy(src, dst, send_sem, recv_sem, k):
-    return remote(src, dst.at[k - 1], send_sem.at[k - 1], recv_sem.at[k - 1], depth_partner(k))
-
-
-def depth_start(src, dst, send_sem, recv_sem):
-    for k in (2, 1, 3):
-        depth_copy(src, dst, send_sem, recv_sem, k).start()
-
-
-def depth_total(src, dst, send_sem, recv_sem):
-    for k in (1, 3, 2):
-        depth_copy(src, dst, send_sem, recv_sem, k).wait_recv()
-    return src[...] + dst[0] + dst[1] + dst[2]
-
-
-def depth_finish(src, dst, send_sem, recv_sem):
-    for k in (1, 2, 3):
-        depth_copy(src, dst, send_sem, recv_sem, k).wait_send()
+    )(
+        d_query,
+        block_sums,
+        own_terms,
+        passage_norm,
+        inverses,
+        query_hidden,
+        passage_hidden,
+        head_weight,
+    )
 
 
 def front_kernel(
@@ -720,95 +923,25 @@
     )(query_hidden, passage_hidden, head_weight, wanted, positions)
 
 
-def to_pieces(blocks, row_groups, feature_groups):
-    count, rows, cols = blocks.shape
-    parts = blocks.reshape(
-        count, row_groups, rows // row_groups, feature_groups, cols // feature_groups
-    )
-    return parts.transpose(1, 3, 0, 2, 4).reshape(
-        row_groups * feature_groups, count, rows // row_groups, cols // feature_groups
-    )
-
-
-def from_pieces(pieces, row_groups, feature_groups):
-    _, count, rows, cols = pieces.shape
-    parts = pieces.reshape(row_groups, feature_groups, count, rows, cols)
-    return parts.transpose(2, 0, 3, 1, 4).reshape(count, row_groups * rows, feature_groups * cols)
-
-
 def local(query_hidden, passage_hidden, head_weight, neg_blocks, pos_ids):
-    dp_count = lax.axis_size("dp")
-    block_count, neg_count = neg_blocks.shape
-    row_count = query_hidden.shape[0]
-    block_rows = row_count // block_count
-    embed_width = head_weight.shape[1]
-    cand_rows = (1 + neg_count) * block_rows
-    request_count = block_count * neg_count
-    total_blocks = dp_count * block_count
-    feature_groups = 4
-    row_groups = dp_count // feature_groups
-    piece_rows = block_rows // row_groups
-    piece_cols = embed_width // feature_groups
-    (
-        attention_probabilities,
-        losses,
-        query_blocks,
-        passage_blocks,
+    weights, losses, query_norm, passage_norm, inverses, fetched, table = front(
+        query_hidden, passage_hidden, head_weight, neg_blocks, pos_ids
+    )
+    d_query, own_terms, returned, query_grad = back(
+        weights, query_norm, passage_norm, fetched, inverses, head_weight
+    )
+    block_sums = add_returned(table[:, :, 0].reshape(512), returned.reshape(512, 16, 256))
+    grad_weight, passage_grad = tail(
+        d_query,
+        block_sums,
+        own_terms,
+        passage_norm,
         inverses,
-        fetched,
-        wanted_table,
-    ) = front(query_hidden, passage_hidden, head_weight, neg_blocks, pos_ids)
-    all_wanted = wanted_table[:, :, 0].reshape(dp_count * request_count)
-    losses = losses[:, 0]
-    passage_inv = inverses[0, :4].reshape(row_count)
-    query_inv = inverses[1, :4].reshape(row_count)
-    query_unit = query_blocks.reshape(row_count, embed_width).astype(jnp.float32)
-    passage_unit = passage_blocks.reshape(row_count, embed_width).astype(jnp.float32)
-    retrieved_documents = jnp.concatenate(
-        [passage_blocks[:, None], fetched.reshape(block_count, neg_count, block_rows, embed_width)],
-        axis=1,
-    ).reshape(block_count, cand_rows, embed_width)
-    d_query = jnp.einsum(
-        "bqc,bce->bqe",
-        attention_probabilities,
-        retrieved_documents,
-        preferred_element_type=jnp.float32,
-    ).reshape(row_count, embed_width)
-    d_cand = jnp.einsum(
-        "bqc,bqe->bce", attention_probabilities, query_blocks, preferred_element_type=jnp.float32
-    )
-    own_terms = d_cand[:, :block_rows]
-    neg_terms = (
-        d_cand[:, block_rows:].reshape(request_count, block_rows, embed_width).astype(jnp.bfloat16)
-    )
-    outgoing = to_pieces(neg_terms, row_groups, feature_groups)
-    returned = lax.all_to_all(outgoing, "dp", split_axis=0, concat_axis=0, tiled=True)
-    selector = (
-        all_wanted[None, :] == jnp.arange(total_blocks, dtype=jnp.int32)[:, None]
-    ).astype(jnp.bfloat16)
-    summed = jnp.dot(
-        selector,
-        returned.reshape(dp_count * request_count, piece_rows * piece_cols),
-        preferred_element_type=jnp.float32,
-    ).astype(jnp.bfloat16)
-    summed = summed.reshape(dp_count, block_count, piece_rows, piece_cols)
-    home = lax.all_to_all(summed, "dp", split_axis=0, concat_axis=0, tiled=True)
-    d_passage = own_terms + from_pieces(home, row_groups, feature_groups).astype(jnp.float32)
-    d_passage = d_passage.reshape(row_count, embed_width)
-    query_inner = lax.psum(jnp.sum(query_unit * d_query, axis=1), "mp")
-    passage_inner = lax.psum(jnp.sum(passage_unit * d_passage, axis=1), "mp")
-    d_query_embed = back_norm(query_inv, query_unit, d_query, query_inner)
-    d_passage_embed = back_norm(passage_inv, passage_unit, d_passage, passage_inner)
-    query_grad = hidden_grad(d_query_embed, head_weight)
-    grad_weight, passage_grad = tail(
-        d_query_embed, d_passage_embed, query_hidden, passage_hidden, head_weight
-    )
-    return (
-        losses.reshape(row_count),
-        grad_weight,
-        query_grad,
-        passage_grad,
-    )
+        query_hidden,
+        passage_hidden,
+        head_weight,
+    )
+    return losses[:, 0].reshape(512), grad_weight, query_grad, passage_grad
 
 
 def solution(mesh):

time: 360 us -> 270 us (0.75)
  waiting for transfers between devices: 60.6 us -> 0 us
  Pallas kernels: 215 us -> 258 us
  local copies, waits for them, and re-layouts: 43.5 us -> 10.1 us
  starting transfers between devices: 15 us -> 0 us
  other arithmetic: 12 us -> 1.26 us
  blocking collectives: 6.78 us -> 0 us
  matrix products: 6.1 us -> 0 us
    all_to_all x2 -> x0, waiting for transfers between devices: 60.6 us -> none  [the longest x1 50 us: local(): lax.all_to_all(outgoing, 'dp', split_axis=0, concat_axis=0, tiled=True)]
    pallas_call x1 -> x2, Pallas kernels: 51.8 us -> 74.6 us  [the longest x1 68.9 us: back(): pl.pallas_call(back_kernel, out_shape=(jax.ShapeDtypeStruct((512, width),...]
    pallas_call x1, Pallas kernels: 55.3 us -> 75.5 us  [tail(): pl.pallas_call(tail_kernel, out_shape=(jax.ShapeDtypeStruct((share, width...]
    convert_element_type x4 -> x0, local copies, waits for them, and re-layouts: 19.2 us -> none  [the longest x2 12.8 us: local(): d_cand[:, block_rows:].reshape(request_count, block_rows, embed_width)]
    all_to_all x2 -> x0, starting transfers between devices: 15 us -> none  [the longest x1 7.83 us: local(): lax.all_to_all(outgoing, 'dp', split_axis=0, concat_axis=0, tiled=True)]
    unnamed x27 -> x5, local copies, waits for them, and re-layouts: 18.3 us -> 5.12 us
    psum x1 -> x0, blocking collectives: 6.78 us -> none  [local(): query_inner = lax.psum(jnp.sum(query_unit * d_query, axis=1), 'mp')]
    dot_general x3 -> x0, matrix products: 6.1 us -> none  [the longest x1 2.99 us: local(): jnp.einsum('bqc,bqe->bce', attention_probabilities, query_blocks, preferr...]
  transfers between devices with their start and end apart: 2 -> 0, of which waited for: 2 -> 0; matrix products, arithmetic and copies ran while one was open for 2% -> 0% of each run, Pallas kernels for 0% -> 0%
where the time goes in v4:
time: 270 us
  Pallas kernels  258 us (96%)
  local copies, waits for them, and re-layouts  10.1 us (4%)
    pallas_call x1, Pallas kernels, front(): pl.pallas_call(front_kernel, out_shape=(jax.ShapeDtypeStruct((4, 128, 640...  108 us
    pallas_call x1, Pallas kernels, tail(): pl.pallas_call(tail_kernel, out_shape=(jax.ShapeDtypeStruct((share, width...  75.5 us
    pallas_call x1, Pallas kernels, back(): pl.pallas_call(back_kernel, out_shape=(jax.ShapeDtypeStruct((512, width),...  68.9 us
    pallas_call x1, Pallas kernels, add_returned(): pl.pallas_call(add_kernel, out_shape=jax.ShapeDtypeStruct((128, 16, 256),...  5.68 us

profile of v4, /device:TPU:1, one launch (start us, length us, event | category | flops | bytes accessed | tf_op | source)
XLA Modules:
  0.0 269.8 jit_solution(6953864075719643880)
XLA Ops:
  0.6 0.8 broadcast_in_dim.7
  1.4 1.3 convert_bitcast_fusion.positions
  2.7 0.7 broadcast_in_dim.8.wanted
  3.3 107.7 %front.1 = (bf16[4,128,640]{2,1,0:T(8,128)(2,1)}, f32[4,8,128]{2,1,0:T(8,128)}, bf16[4,128,1024]{2,1,0:T(8,128)(2,1)}, bf16[4,128,1024]{2,1,0:T(8,128)(2,1)}, f3...) custom-call(bf16[512,4096]{1,0:T(8,128)(2,1)} %query_hbm.3, ...), custom_call_target="tpu_custom_call" | custom-call | tf_op jit(solution)/shard_map/front/pallas_call | solution.py:878
  111.0 1.3 slice.6
  112.3 1.6 slice_reduce_fusion
  113.9 0.7 reshape_squeeze.7.table
  114.5 68.9 %back.1 = (bf16[512,1024]{1,0:T(8,128)(2,1)}, f32[4,128,1024]{2,1,0:T(8,128)}, bf16[32,16,16,256]{3,2,1,0:T(8,128)(2,1)}, bf16[512,1024]{1,0:T(8,128)(2,1)}) custom-call(bf16[4,128,640]{2,1,0:T(8,128)(2,1)} %get-tuple-element.18.weights, bf16[4,128,1024]{2,1,0:T(8,128)(2,1)} %get-tuple-element.19.query_norm, ...), custom_call_target="tpu_custom_call" | custom-call | tf_op jit(solution)/shard_map/back/pallas_call | solution.py:270
  183.4 5.7 %add_returned.1.block_sums = bf16[128,16,256]{2,1,0:T(8,128)(2,1)} custom-call(s32[512]{0:T(512)} %reshape_squeeze.7.table, bf16[512,16,256]{2,1,0:T(8,128)(2,1)} %bitcast.4), custom_call_target="tpu_custom_call" | custom-call | tf_op jit(solution)/shard_map/add_returned/pallas_call | solution.py:316
  189.1 0.0 copy-start
  189.1 75.5 %tail.1 = (f32[128,1024]{1,0:T(8,128)}, bf16[512,1024]{1,0:T(8,128)(2,1)}) custom-call(bf16[512,1024]{1,0:T(8,128)(2,1)} %get-tuple-element.23.d_query, bf16[128,16,256]{2,1,0:T(8,128)(2,1)} %add_returned.1.block_sums, f32[4,128,1024]{2,1,0:T(8,128)} %get-tuple-element.26.own_terms, bf16[4,128,1024]{2,1,0:T(8,128)(2,1)} %get-tuple-element.20.passage_norm, ...), custom_call_target="tpu_custom_call" | custom-call | tf_op jit(solution)/shard_map/tail/pallas_call | solution.py:590
  264.7 1.9 copy.12
  266.6 0.0 copy-done
  266.6 1.0 copy.13
  267.5 2.3 copy.14
Async XLA Ops:
  189.1 77.4 %copy-start = (bf16[512,1024]{1,0:T(8,128)(2,1)S(1)}, bf16[512,1024]{1,0:T(8,128)(2,1)}, u32[]{:S(2)}) copy-start(bf16[512,1024]{1,0:T(8,128)(2,1)} %get-tuple-element.36) | copy-start | bytes 3145732

commit v5 on v4

--- a/solution.py
+++ b/solution.py
@@ -45,46 +45,81 @@
     )
 
 
-def hidden_send(part, landed, send_sem, recv_sem, k):
-    return remote(
-        part.at[k], landed.at[k - 1], send_sem.at[k - 1], recv_sem.at[k - 1], depth_partner(k)
-    )
+def hidden_send(part, early_in, final_in, send_sem, recv_sem, side, stage):
+    half = part.shape[1] // 2
+    merged_rows = pl.ds(side * half, half)
+    plain_rows = pl.ds((1 - side) * half, half)
+    near = (1, 3)[side]
+    if stage == 0:
+        src, dst = part.at[2, merged_rows], early_in.at[side]
+    elif stage == 1:
+        src, dst = part.at[near, plain_rows], final_in.at[side, plain_rows]
+    else:
+        src, dst = part.at[near, merged_rows], final_in.at[side, merged_rows]
+    return remote(src, dst, send_sem.at[side, stage], recv_sem.at[side, stage], depth_partner(near))
 
 
 DEPTH_ORDER = (2, 1, 3, 0)
 
 
-def hidden_parts(grad, head_hbm, head, part, landed, load_sem, send_sem, recv_sem):
+def hidden_parts(grad, head_of, part, early_in, final_in, send_sem, recv_sem):
+    half = grad.shape[0] // 2
+    sends = (part, early_in, final_in, send_sem, recv_sem)
     for k in DEPTH_ORDER:
-        head_load(head_hbm, head, load_sem, k).wait()
-        half = grad.shape[0] // 2
+        head = head_of(k)
 
         @pl.loop(0, 2)
         def _(i):
             rows = pl.ds(pl.multiple_of(i * half, half), half)
             part[k, rows] = lax.dot_general(
-                grad[rows], head[k], COL_CONTRACT, preferred_element_type=jnp.float32
+                grad[rows], head[...], COL_CONTRACT, preferred_element_type=jnp.float32
             ).astype(jnp.bfloat16)
 
-        if k:
-            hidden_send(part, landed, send_sem, recv_sem, k).start()
-
-
-def hidden_sum(part, landed, send_sem, recv_sem, out):
-    for k in (1, 3, 2):
-        hidden_send(part, landed, send_sem, recv_sem, k).wait_recv()
-    rows_step = 64
-
-    @pl.loop(0, out.shape[0] // rows_step)
+        if k == 2:
+            hidden_send(*sends, 0, 0).start()
+            hidden_send(*sends, 1, 0).start()
+        elif k:
+            hidden_send(*sends, k // 2, 1).start()
+
+
+def hidden_merge(part, early_in, final_in, send_sem, recv_sem):
+    half = part.shape[1] // 2
+    step = 64
+    for side in range(2):
+        hidden_send(part, early_in, final_in, send_sem, recv_sem, side, 0).wait_recv()
+        near = (1, 3)[side]
+
+        @pl.loop(0, half // step)
+        def _(i):
+            rows = pl.ds(pl.multiple_of(side * half + i * step, step), step)
+            early_rows = pl.ds(pl.multiple_of(i * step, step), step)
+            part[near, rows] = (
+                part[near, rows].astype(jnp.float32)
+                + early_in[side, early_rows].astype(jnp.float32)
+            ).astype(jnp.bfloat16)
+
+        hidden_send(part, early_in, final_in, send_sem, recv_sem, side, 2).start()
+
+
+def hidden_sum(part, early_in, final_in, send_sem, recv_sem, out):
+    step = 64
+    sends = (part, early_in, final_in, send_sem, recv_sem)
+    for stage in (1, 2):
+        for side in range(2):
+            hidden_send(*sends, side, stage).wait_recv()
+
+    @pl.loop(0, out.shape[0] // step)
     def _(i):
-        rows = pl.ds(pl.multiple_of(i * rows_step, rows_step), rows_step)
-        total = part[0, rows].astype(jnp.float32)
-        for k in range(3):
-            total = total + landed[k, rows].astype(jnp.float32)
-        out[rows] = total.astype(jnp.bfloat16)
-
-    for k in (1, 3, 2):
-        hidden_send(part, landed, send_sem, recv_sem, k).wait_send()
+        rows = pl.ds(pl.multiple_of(i * step, step), step)
+        out[rows] = (
+            part[0, rows].astype(jnp.float32)
+            + final_in[0, rows].astype(jnp.float32)
+            + final_in[1, rows].astype(jnp.float32)
+        ).astype(jnp.bfloat16)
+
+    for stage in range(3):
+        for side in range(2):
+            hidden_send(*sends, side, stage).wait_send()
 
 
 def place():
@@ -157,147 +192,10 @@
         depth_copy(src, dst, send_sem, recv_sem, k).wait_send()
 
 
-def back_kernel(
-    weights,
-    query_norm,
-    passage_norm,
-    fetched,
-    inverses,
-    head_hbm,
-    d_query_embed,
-    own_terms,
-    returned,
-    hidden_out,
-    head,
-    d_query,
-    outgoing,
-    part,
-    landed,
-    inner,
-    inner_in,
-    load_sem,
-    depth_send,
-    depth_recv,
-    return_send,
-    return_recv,
-    inner_send,
-    inner_recv,
-):
-    dp = lax.axis_index("dp")
-    width = head.shape[1]
-    for k in DEPTH_ORDER:
-        head_load(head_hbm, head, load_sem, k).start()
-    greet(
-        [{"dp": plane_peer(offset)} for offset in OFFSETS]
-        + [depth_partner(k) for k in (1, 2, 3)]
-    )
-
-    @pl.loop(0, 4)
-    def _(b):
-        outgoing[pl.ds(b * 4, 4)] = (
-            lax.dot_general(
-                weights[b, :, 128:],
-                query_norm[b],
-                ROW_CONTRACT,
-                preferred_element_type=jnp.float32,
-            )
-            .astype(jnp.bfloat16)
-            .reshape(4, 128, width)
-        )
-
-    def return_copy(j):
-        peer = plane_peer(OFFSETS[j])
-        return remote(
-            outgoing.at[:, share_rows(peer), share_cols(peer)],
-            returned.at[dp],
-            return_send.at[j],
-            return_recv.at[j],
-            {"dp": peer},
-        )
-
-    for j in range(31):
-        return_copy(j).start()
-    returned[dp] = outgoing[:, share_rows(dp), share_cols(dp)]
-    inner[4:8] = jnp.zeros((4, 128), jnp.float32)
-
-    for b in range(4):
-        total = jnp.dot(
-            weights[b, :, :128], passage_norm[b], preferred_element_type=jnp.float32
-        ) + jnp.dot(
-            weights[b, :, 128:],
-            fetched[4 * b : 4 * b + 4].reshape(512, width),
-            preferred_element_type=jnp.float32,
-        )
-        d_query[b] = total
-        inner[b : b + 1] = as_row(
-            jnp.sum(query_norm[b].astype(jnp.float32) * total, axis=1, keepdims=True)
-        )
-    inner_args = (inner, inner_in, inner_send, inner_recv)
-    depth_start(*inner_args)
-
-    @pl.loop(0, 4)
-    def _(b):
-        own_terms[b] = lax.dot_general(
-            weights[b, :, :128], query_norm[b], ROW_CONTRACT, preferred_element_type=jnp.float32
-        )
-
-    total_inner = depth_total(*inner_args)
-    for b in range(4):
-        d_query_embed[b * 128 : (b + 1) * 128] = embed_grad(
-            inverses[1, b : b + 1], query_norm[b], d_query[b], total_inner[b : b + 1]
-        )
-    hidden_parts(d_query_embed, head_hbm, head, part, landed, load_sem, depth_send, depth_recv)
-    hidden_sum(part, landed, depth_send, depth_recv, hidden_out)
-    for j in range(31):
-        return_copy(j).wait_recv()
-    depth_finish(*inner_args)
-    for j in range(31):
-        return_copy(j).wait_send()
-
-
 def embed_grad(inverse_row, unit, d_unit, inner_row):
     return (
         as_column(inverse_row) * (d_unit - unit.astype(jnp.float32) * as_column(inner_row))
     ).astype(jnp.bfloat16)
-
-
-def back(weights, query_norm, passage_norm, fetched, inverses, head_weight):
-    bf16 = jnp.bfloat16
-    f32 = jnp.float32
-    width = head_weight.shape[1]
-    vmem = pl.BlockSpec(memory_space=pltpu.VMEM)
-    dma = pltpu.SemaphoreType.DMA
-    return pl.pallas_call(
-        back_kernel,
-        out_shape=(
-            jax.ShapeDtypeStruct((512, width), bf16),
-            jax.ShapeDtypeStruct((4, 128, width), f32),
-            jax.ShapeDtypeStruct((32, 16, 16, 256), bf16),
-            jax.ShapeDtypeStruct((512, width), bf16),
-        ),
-        in_specs=[vmem] * 5 + [pl.BlockSpec(memory_space=pl.ANY)],
-        out_specs=(vmem,) * 4,
-        scratch_shapes=[
-            pltpu.VMEM((4, width, width), bf16),
-            pltpu.VMEM((4, 128, width), f32),
-            pltpu.VMEM((16, 128, width), bf16),
-            pltpu.VMEM((4, 512, width), bf16),
-            pltpu.VMEM((3, 512, width), bf16),
-            pltpu.VMEM((8, 128), f32),
-            pltpu.VMEM((3, 8, 128), f32),
-            dma((4,)),
-            dma((3,)),
-            dma((3,)),
-            dma((31,)),
-            dma((31,)),
-            dma((3,)),
-            dma((3,)),
-        ],
-        compiler_params=pltpu.CompilerParams(
-            collective_id=1, has_side_effects=True, vmem_limit_bytes=VMEM_LIMIT
-        ),
-        name="back",
-    )(weights, query_norm, passage_norm, fetched, inverses, head_weight)
 
 
 def add_kernel(table, returned, out, total):
@@ -353,7 +251,8 @@
     second_out,
     second_in,
     part,
-    landed,
+    early_in,
+    final_in,
     load_sem,
     hidden_load_sem,
     depth_send,
@@ -423,7 +322,10 @@
         d_passage[b * 128 : (b + 1) * 128] = embed_grad(
             inverses[0, b : b + 1], passage_norm[b], d_total[b], total_inner[b : b + 1]
         )
-    hidden_parts(d_passage, head_hbm, head, part, landed, load_sem, depth_send, depth_recv)
+    for k in DEPTH_ORDER:
+        head_load(head_hbm, head, load_sem, k).wait()
+    depth_args = (part, early_in, final_in, depth_send, depth_recv)
+    hidden_parts(d_passage, lambda k: head.at[k], *depth_args)
 
     def core_copy(chip):
         return remote(
@@ -499,6 +401,10 @@
 
     @pl.loop(0, 9)
     def _(i):
+        @pl.when(i == 4)
+        def _():
+            hidden_merge(*depth_args)
+
         @pl.when(i < 8)
         def _():
             produce(i)
@@ -550,7 +456,7 @@
             weight_out[:, side * half : (side + 1) * half] += second_in[side, k - 1].astype(
                 jnp.float32
             )
-    hidden_sum(part, landed, depth_send, depth_recv, hidden_out)
+    hidden_sum(*depth_args, hidden_out)
     for j in range(31):
         home_copy(j).wait_send()
     depth_finish(*inner_args)
@@ -615,11 +521,12 @@
             pltpu.VMEM((2, 3, share, width // 2), bf16),
             pltpu.VMEM((2, 3, share, width // 2), bf16),
             pltpu.VMEM((4, rows, width), bf16),
-            pltpu.VMEM((3, rows, width), bf16),
+            pltpu.VMEM((2, rows // 2, width), bf16),
+            pltpu.VMEM((2, rows, width), bf16),
             dma((4,)),
             dma((2, 2)),
-            dma((3,)),
-            dma((3,)),
+            dma((2, 3)),
+            dma((2, 3)),
             dma((16,)),
             dma((16,)),
             dma((2, 16)),
@@ -643,29 +550,41 @@
     )
 
 
-def front_kernel(
+def main_kernel(
     query_hbm,
     passage_hbm,
     head_hbm,
-    wanted,
+    negatives,
     positions,
-    weights,
     losses,
-    query_norm,
     passage_norm,
     inverses,
-    fetched,
-    all_wanted,
+    table,
+    d_query_embed,
+    own_terms,
+    returned,
+    hidden_out,
     head,
     hidden,
     embed,
+    query_norm,
+    wanted,
+    all_wanted,
+    wanted_smem,
+    targets,
     held,
     reply,
+    fetched,
     partial,
     partial_in,
+    weights,
+    loss_rows,
+    outgoing,
+    part,
+    early_in,
+    final_in,
     squares,
     squares_in,
-    table,
     load_sem,
     table_sem,
     square_send,
@@ -676,17 +595,22 @@
     spread_recv,
     reply_send,
     reply_recv,
+    return_send,
+    return_recv,
     partial_send,
     partial_recv,
     weight_send,
     weight_recv,
     loss_send,
     loss_recv,
+    depth_send,
+    depth_recv,
 ):
     dp = lax.axis_index("dp")
     mp = lax.axis_index("mp")
     depth = head.shape[1]
     hidden_hbm = (passage_hbm, query_hbm)
+    my_rows = pl.ds(pl.multiple_of(mp * 32, 32), 32)
 
     def hidden_load(side, chunk):
         columns = pl.ds(pl.multiple_of(chunk * depth, depth), depth)
@@ -703,6 +627,8 @@
         head_chunk(chunk).start()
     for chunk in range(4):
         hidden_load(1, chunk).start()
+    for i in range(16):
+        wanted[i : i + 1] = jnp.full((1, 128), negatives[i // 4, i % 4], jnp.int32)
     embed[...] = jnp.zeros_like(embed)
     greet(
         [{"dp": plane_peer(offset)} for offset in OFFSETS]
@@ -721,6 +647,8 @@
     for j in range(31):
         want_copy(j).start()
     all_wanted[dp] = wanted[...]
+    for b in range(4):
+        targets[b] = jnp.broadcast_to(as_column(positions[b : b + 1]), (128, 128))
 
     def project(side):
         @pl.loop(0, 4)
@@ -773,164 +701,279 @@
     normalize(1, query_norm)
     for j in range(31):
         want_copy(j).wait_recv()
-    table_copy = pltpu.make_async_copy(all_wanted, table, table_sem)
+    table_copy = pltpu.make_async_copy(all_wanted, wanted_smem, table_sem)
     table_copy.start()
     table_copy.wait()
     for j in range(31):
         spread_copy(j).wait_recv()
 
-    def reply_copy(j):
+    def four(b):
+        return pl.ds(b * 4, 4)
+
+    def reply_copy(j, b):
         peer = plane_peer(OFFSETS[j])
         return remote(
-            reply.at[peer],
-            fetched.at[:, share_rows(dp), share_cols(dp)],
-            reply_send.at[j],
-            reply_recv.at[j],
+            reply.at[peer, four(b)],
+            fetched.at[four(b), share_rows(dp), share_cols(dp)],
+            reply_send.at[j, b],
+            reply_recv.at[j, b],
             {"dp": peer},
         )
 
-    def gather(device):
-        @pl.loop(0, 16, unroll=4)
-        def _(i):
-            reply[device, i] = held[table[device, i, 0]]
-
-    for j in range(31):
-        gather(plane_peer(OFFSETS[j]))
-        reply_copy(j).start()
-    gather(dp)
-    fetched[:, share_rows(dp), share_cols(dp)] = reply[dp]
-    for j in range(31):
-        reply_copy(j).wait_recv()
-
-    def partial_copy(k):
+    def gather(device, b):
+        for i in range(4):
+            reply[device, b * 4 + i] = held[wanted_smem[device, b * 4 + i, 0]]
+
+    @pl.loop(0, 4)
+    def _(b):
+        for j in range(31):
+            gather(plane_peer(OFFSETS[j]), b)
+            reply_copy(j, b).start()
+        gather(dp, b)
+        fetched[four(b), share_rows(dp), share_cols(dp)] = reply[dp, four(b)]
+
+    @pl.loop(0, 32)
+    def _(device):
+        for i in range(16):
+            table[device * 16 + i] = wanted_smem[device, i, 0]
+
+    def partial_copy(b, k):
+        peer_rows = pl.ds(pl.multiple_of(lax.rem(mp + k, 4) * 32, 32), 32)
         return depth_copy(
-            partial.at[lax.rem(mp + k, 4)], partial_in, partial_send, partial_recv, k
-        )
-
-    for k in DEPTH_ORDER:
-        b = lax.rem(mp + k, 4)
+            partial.at[b, peer_rows], partial_in.at[b], partial_send.at[b], partial_recv.at[b], k
+        )
+
+    def score(b):
+        for j in range(31):
+            reply_copy(j, b).wait_recv()
         rows = query_norm[b]
         partial[b, :, :128] = lax.dot_general(
             rows, passage_norm[b], COL_CONTRACT, preferred_element_type=jnp.float32
         ).astype(jnp.bfloat16)
-        others = fetched[pl.ds(b * 4, 4)].reshape(512, depth)
+        others = fetched[four(b)].reshape(512, depth)
         partial[b, :, 128:] = lax.dot_general(
             rows, others, COL_CONTRACT, preferred_element_type=jnp.float32
         ).astype(jnp.bfloat16)
-        if k:
-            partial_copy(k).start()
-    scores = partial[mp].astype(jnp.float32)
+        for k in (2, 1, 3):
+            partial_copy(b, k).start()
+
+    def weight_copy(b, k):
+        return remote(
+            weights.at[b, my_rows],
+            weights.at[b, my_rows],
+            weight_send.at[b, k - 1],
+            weight_recv.at[b, k - 1],
+            depth_partner(k),
+        )
+
+    def weigh(b):
+        scores = partial[b, my_rows].astype(jnp.float32)
+        for k in (1, 3, 2):
+            partial_copy(b, k).wait_recv()
+            scores = scores + partial_in[b, k - 1].astype(jnp.float32)
+        scores = scores / logit_divisor
+        columns = lax.broadcasted_iota(jnp.int32, scores.shape, 1).astype(jnp.float32)
+        matching = (columns == targets[b, my_rows][:, :1]).astype(jnp.float32)
+        powers = jnp.exp(scores)
+        totals = jnp.sum(powers, axis=1, keepdims=True)
+        loss = jnp.log(totals) - jnp.sum(scores * matching, axis=1, keepdims=True)
+        weights[b, my_rows] = ((powers / totals - matching) / logit_divisor).astype(jnp.bfloat16)
+        loss_rows[b, my_rows] = jnp.broadcast_to(loss, (32, 128))
+        for k in (2, 1, 3):
+            weight_copy(b, k).start()
+
+    def return_copy(j, b):
+        peer = plane_peer(OFFSETS[j])
+        return remote(
+            outgoing.at[four(b), share_rows(peer), share_cols(peer)],
+            returned.at[dp, four(b)],
+            return_send.at[j, b],
+            return_recv.at[j, b],
+            {"dp": peer},
+        )
+
+    def give_back(b):
+        for k in (1, 3, 2):
+            weight_copy(b, k).wait_recv()
+        outgoing[four(b)] = (
+            lax.dot_general(
+                weights[b, :, 128:],
+                query_norm[b],
+                ROW_CONTRACT,
+                preferred_element_type=jnp.float32,
+            )
+            .astype(jnp.bfloat16)
+            .reshape(4, 128, depth)
+        )
+        for j in range(31):
+            return_copy(j, b).start()
+        returned[dp, four(b)] = outgoing[four(b), share_rows(dp), share_cols(dp)]
+        total = jnp.dot(
+            weights[b, :, :128], passage_norm[b], preferred_element_type=jnp.float32
+        ) + jnp.dot(
+            weights[b, :, 128:],
+            fetched[four(b)].reshape(512, depth),
+            preferred_element_type=jnp.float32,
+        )
+        embed[0, pl.ds(pl.multiple_of(b * 128, 128), 128)] = total
+        squares[2, pl.ds(b, 1)] = as_row(
+            jnp.sum(query_norm[b].astype(jnp.float32) * total, axis=1, keepdims=True)
+        )
+        own_terms[b] = lax.dot_general(
+            weights[b, :, :128], query_norm[b], ROW_CONTRACT, preferred_element_type=jnp.float32
+        )
+
+    squares[2, 4:8] = jnp.zeros((4, 128), jnp.float32)
+
+    @pl.loop(0, 6)
+    def _(step):
+        @pl.when(step < 4)
+        def _():
+            score(step)
+
+        @pl.when((step >= 1) & (step < 5))
+        def _():
+            weigh(step - 1)
+
+        @pl.when(step >= 2)
+        def _():
+            give_back(step - 2)
+
+    depth_start(*square_args(2))
+
+    def loss_copy(k):
+        return remote(
+            loss_rows.at[:, my_rows],
+            loss_rows.at[:, my_rows],
+            loss_send.at[k - 1],
+            loss_recv.at[k - 1],
+            depth_partner(k),
+        )
+
+    for k in (2, 1, 3):
+        loss_copy(k).start()
+    inner = depth_total(*square_args(2))
+    for b in range(4):
+        d_query_embed[b * 128 : (b + 1) * 128] = embed_grad(
+            inverses[1, b : b + 1],
+            query_norm[b],
+            embed[0, b * 128 : (b + 1) * 128],
+            inner[b : b + 1],
+        )
+    depth_args = (part, early_in, final_in, depth_send, depth_recv)
+    hidden_parts(d_query_embed, lambda k: head.at[lax.rem(mp + k, 4)], *depth_args)
     for k in (1, 3, 2):
-        partial_copy(k).wait_recv()
-        scores = scores + partial_in[k - 1].astype(jnp.float32)
-    scores = scores / logit_divisor
-    columns = lax.broadcasted_iota(jnp.int32, scores.shape, 1).astype(jnp.float32)
-    matching = (columns == as_column(positions[pl.ds(mp, 1)])).astype(jnp.float32)
-    powers = jnp.exp(scores)
-    totals = jnp.sum(powers, axis=1, keepdims=True)
-    loss = jnp.log(totals) - jnp.sum(scores * matching, axis=1, keepdims=True)
-    weights[mp] = ((powers / totals - matching) / logit_divisor).astype(jnp.bfloat16)
-    losses[mp] = jnp.broadcast_to(as_row(loss), (8, 128))
-
-    def weight_copies(k):
-        return (
-            remote(
-                weights.at[mp],
-                weights.at[mp],
-                weight_send.at[k - 1],
-                weight_recv.at[k - 1],
-                depth_partner(k),
-            ),
-            remote(
-                losses.at[mp],
-                losses.at[mp],
-                loss_send.at[k - 1],
-                loss_recv.at[k - 1],
-                depth_partner(k),
-            ),
-        )
-
-    for k in (2, 1, 3):
-        for copy in weight_copies(k):
-            copy.start()
+        loss_copy(k).wait_recv()
+    for b in range(4):
+        losses[b : b + 1] = as_row(loss_rows[b, :, :1])
+    hidden_merge(*depth_args)
     for j in range(31):
         want_copy(j).wait_send()
         spread_copy(j).wait_send()
-        reply_copy(j).wait_send()
-    depth_finish(*square_args(0))
-    depth_finish(*square_args(1))
-    for k in (1, 3, 2):
-        partial_copy(k).wait_send()
-        for copy in weight_copies(k):
-            copy.wait()
-
-
-def front(query_hidden, passage_hidden, head_weight, neg_blocks, pos_ids):
+    for side in range(3):
+        depth_finish(*square_args(side))
+    for k in (1, 2, 3):
+        loss_copy(k).wait_send()
+
+    @pl.loop(0, 4)
+    def _(b):
+        for k in (1, 2, 3):
+            partial_copy(b, k).wait_send()
+            weight_copy(b, k).wait_send()
+        for j in range(31):
+            reply_copy(j, b).wait_send()
+            return_copy(j, b).wait_send()
+            return_copy(j, b).wait_recv()
+
+    hidden_sum(*depth_args, hidden_out)
+
+
+def main_part(query_hidden, passage_hidden, head_weight, neg_blocks, pos_ids):
     bf16 = jnp.bfloat16
     f32 = jnp.float32
     rows = query_hidden.shape[0]
     width = head_weight.shape[1]
-    wanted = jnp.broadcast_to(neg_blocks.reshape(16, 1), (16, 128))
     positions = pos_ids.reshape(4, 128).astype(f32)
     vmem = pl.BlockSpec(memory_space=pltpu.VMEM)
+    smem = pl.BlockSpec(memory_space=pltpu.SMEM)
     hbm = pl.BlockSpec(memory_space=pl.ANY)
     dma = pltpu.SemaphoreType.DMA
     return pl.pallas_call(
-        front_kernel,
+        main_kernel,
         out_shape=(
-            jax.ShapeDtypeStruct((4, 128, 640), bf16),
-            jax.ShapeDtypeStruct((4, 8, 128), f32),
-            jax.ShapeDtypeStruct((4, 128, width), bf16),
+            jax.ShapeDtypeStruct((4, 128), f32),
             jax.ShapeDtypeStruct((4, 128, width), bf16),
             jax.ShapeDtypeStruct((2, 8, 128), f32),
-            jax.ShapeDtypeStruct((16, 128, width), bf16),
-            jax.ShapeDtypeStruct((32, 16, 128), jnp.int32),
+            jax.ShapeDtypeStruct((512,), jnp.int32),
+            jax.ShapeDtypeStruct((rows, width), bf16),
+            jax.ShapeDtypeStruct((4, 128, width), f32),
+            jax.ShapeDtypeStruct((32, 16, 16, 256), bf16),
+            jax.ShapeDtypeStruct((rows, width), bf16),
         ),
-        in_specs=[hbm, hbm, hbm, vmem, vmem],
-        out_specs=(vmem,) * 7,
+        in_specs=[hbm, hbm, hbm, smem, vmem],
+        out_specs=(vmem, vmem, vmem, smem, vmem, vmem, vmem, vmem),
         scratch_shapes=[
             pltpu.VMEM((4, width, width), bf16),
             pltpu.VMEM((2, 4, rows, width), bf16),
             pltpu.VMEM((2, rows, width), f32),
+            pltpu.VMEM((4, 128, width), bf16),
+            pltpu.VMEM((16, 128), jnp.int32),
+            pltpu.VMEM((32, 16, 128), jnp.int32),
+            pltpu.SMEM((32, 16, 128), jnp.int32),
+            pltpu.VMEM((4, 128, 128), f32),
             pltpu.VMEM((128, 16, 256), bf16),
             pltpu.VMEM((32, 16, 16, 256), bf16),
+            pltpu.VMEM((16, 128, width), bf16),
             pltpu.VMEM((4, 128, 640), bf16),
-            pltpu.VMEM((3, 128, 640), bf16),
-            pltpu.VMEM((2, 8, 128), f32),
-            pltpu.VMEM((2, 3, 8, 128), f32),
-            pltpu.SMEM((32, 16, 128), jnp.int32),
+            pltpu.VMEM((4, 3, 32, 640), bf16),
+            pltpu.VMEM((4, 128, 640), bf16),
+            pltpu.VMEM((4, 128, 128), f32),
+            pltpu.VMEM((16, 128, width), bf16),
+            pltpu.VMEM((4, rows, width), bf16),
+            pltpu.VMEM((2, rows // 2, width), bf16),
+            pltpu.VMEM((2, rows, width), bf16),
+            pltpu.VMEM((3, 8, 128), f32),
+            pltpu.VMEM((3, 3, 8, 128), f32),
             dma((3, 4)),
             dma,
-            dma((2, 3)),
-            dma((2, 3)),
+            dma((3, 3)),
+            dma((3, 3)),
             dma((31,)),
             dma((31,)),
             dma((31,)),
             dma((31,)),
-            dma((31,)),
-            dma((31,)),
+            dma((31, 4)),
+            dma((31, 4)),
+            dma((31, 4)),
+            dma((31, 4)),
+            dma((4, 3)),
+            dma((4, 3)),
+            dma((4, 3)),
+            dma((4, 3)),
             dma((3,)),
             dma((3,)),
-            dma((3,)),
-            dma((3,)),
-            dma((3,)),
-            dma((3,)),
+            dma((2, 3)),
+            dma((2, 3)),
         ],
         compiler_params=pltpu.CompilerParams(
-            collective_id=3, has_side_effects=True, vmem_limit_bytes=VMEM_LIMIT
+            collective_id=1, has_side_effects=True, vmem_limit_bytes=VMEM_LIMIT
         ),
-        name="front",
-    )(query_hidden, passage_hidden, head_weight, wanted, positions)
+        name="main_part",
+    )(query_hidden, passage_hidden, head_weight, neg_blocks, positions)
 
 
 def local(query_hidden, passage_hidden, head_weight, neg_blocks, pos_ids):
-    weights, losses, query_norm, passage_norm, inverses, fetched, table = front(
-        query_hidden, passage_hidden, head_weight, neg_blocks, pos_ids
-    )
-    d_query, own_terms, returned, query_grad = back(
-        weights, query_norm, passage_norm, fetched, inverses, head_weight
-    )
-    block_sums = add_returned(table[:, :, 0].reshape(512), returned.reshape(512, 16, 256))
+    (
+        losses,
+        passage_norm,
+        inverses,
+        table,
+        d_query,
+        own_terms,
+        returned,
+        query_grad,
+    ) = main_part(query_hidden, passage_hidden, head_weight, neg_blocks, pos_ids)
+    block_sums = add_returned(table, returned.reshape(512, 16, 256))
     grad_weight, passage_grad = tail(
         d_query,
         block_sums,
@@ -941,7 +984,7 @@
         passage_hidden,
         head_weight,
     )
-    return losses[:, 0].reshape(512), grad_weight, query_grad, passage_grad
+    return losses.reshape(512), grad_weight, query_grad, passage_grad
 
 
 def solution(mesh):

time: 270 us -> 231 us (0.86)
  Pallas kernels: 258 us -> 224 us
  local copies, waits for them, and re-layouts: 10.1 us -> 5.7 us
    pallas_call x2 -> x1, Pallas kernels: 177 us -> 144 us  [main_part(): pl.pallas_call(main_kernel, out_shape=(jax.ShapeDtypeStruct((4, 128), f32...]
    slice x2 -> x0, local copies, waits for them, and re-layouts: 2.86 us -> none  [the longest x1 1.56 us: local(): table[:, :, 0].reshape(512)]
    unnamed x5 -> x8, local copies, waits for them, and re-layouts: 5.12 us -> 5.7 us
where the time goes in v5:
time: 231 us
  Pallas kernels  224 us (97%)
  local copies, waits for them, and re-layouts  5.7 us (2%)
    pallas_call x1, Pallas kernels, main_part(): pl.pallas_call(main_kernel, out_shape=(jax.ShapeDtypeStruct((4, 128), f32...  144 us
    pallas_call x1, Pallas kernels, tail(): pl.pallas_call(tail_kernel, out_shape=(jax.ShapeDtypeStruct((share, width...  74 us
    unnamed x8, local copies, waits for them, and re-layouts  5.7 us
    pallas_call x1, Pallas kernels, add_returned(): pl.pallas_call(add_kernel, out_shape=jax.ShapeDtypeStruct((128, 16, 256),...  5.49 us

profile of v5, /device:TPU:1, one launch (start us, length us, event | category | flops | bytes accessed | tf_op | source)
XLA Modules:
  0.0 231.1 jit_solution(4177273978661326690)
XLA Ops:
  0.6 1.3 convert_bitcast_fusion.positions
  1.9 144.1 %main_part.1 = (f32[4,128]{1,0:T(4,128)}, bf16[4,128,1024]{2,1,0:T(8,128)(2,1)}, f32[2,8,128]{2,1,0:T(8,128)}, s32[512]{0:T(512)}, bf16[512,1024]{1,0:T(8,128)(2...) custom-call(bf16[512,4096]{1,0:T(8,128)(2,1)} %query_hbm.3, ...), custom_call_target="tpu_custom_call" | custom-call | tf_op jit(solution)/shard_map/main_part/pallas_call | solution.py:901
  146.0 5.5 %add_returned.1.block_sums = bf16[128,16,256]{2,1,0:T(8,128)(2,1)} custom-call(s32[512]{0:T(512)} %get-tuple-element.16.table, bf16[512,16,256]{2,1,0:T(8,128)(2,1)} %bitcast.4), custom_call_target="tpu_custom_call" | custom-call | tf_op jit(solution)/shard_map/add_returned/pallas_call | solution.py:214
  151.4 0.0 copy-start.1
  151.5 0.0 copy-start
  151.5 74.0 %tail.1 = (f32[128,1024]{1,0:T(8,128)}, bf16[512,1024]{1,0:T(8,128)(2,1)}) custom-call(bf16[512,1024]{1,0:T(8,128)(2,1)} %get-tuple-element.15.d_query, bf16[128,16,256]{2,1,0:T(8,128)(2,1)} %add_returned.1.block_sums, f32[4,128,1024]{2,1,0:T(8,128)} %get-tuple-element.18.own_terms, bf16[4,128,1024]{2,1,0:T(8,128)(2,1)} %get-tuple-element.19.passage_norm, ...), custom_call_target="tpu_custom_call" | custom-call | tf_op jit(solution)/shard_map/tail/pallas_call | solution.py:496
  225.4 0.0 copy-done.1
  225.4 0.6 copy.13
  226.0 1.9 copy.14
  227.9 0.0 copy-done
  227.9 1.0 copy.15
  228.9 2.3 copy.16
Async XLA Ops:
  151.4 74.0 %copy-start.1 = (f32[4,128]{1,0:T(4,128)S(1)}, f32[4,128]{1,0:T(4,128)}, u32[]{:S(2)}) copy-start(f32[4,128]{1,0:T(4,128)} %get-tuple-element.14) | copy-start | bytes 6148
  151.5 76.4 %copy-start = (bf16[512,1024]{1,0:T(8,128)(2,1)S(1)}, bf16[512,1024]{1,0:T(8,128)(2,1)}, u32[]{:S(2)}) copy-start(bf16[512,1024]{1,0:T(8,128)(2,1)} %get-tuple-element.30) | copy-start | bytes 3145732

commit v6 on v5

--- a/solution.py
+++ b/solution.py
@@ -62,23 +62,25 @@
 DEPTH_ORDER = (2, 1, 3, 0)
 
 
+def hidden_dot(grad, head, out):
+    half = grad.shape[0] // 2
+
+    @pl.loop(0, 2)
+    def _(i):
+        rows = pl.ds(pl.multiple_of(i * half, half), half)
+        out[rows] = lax.dot_general(
+            grad[rows], head[...], COL_CONTRACT, preferred_element_type=jnp.float32
+        ).astype(jnp.bfloat16)
+
+
 def hidden_parts(grad, head_of, part, early_in, final_in, send_sem, recv_sem):
-    half = grad.shape[0] // 2
     sends = (part, early_in, final_in, send_sem, recv_sem)
-    for k in DEPTH_ORDER:
-        head = head_of(k)
-
-        @pl.loop(0, 2)
-        def _(i):
-            rows = pl.ds(pl.multiple_of(i * half, half), half)
-            part[k, rows] = lax.dot_general(
-                grad[rows], head[...], COL_CONTRACT, preferred_element_type=jnp.float32
-            ).astype(jnp.bfloat16)
-
+    for k in (2, 1, 3):
+        hidden_dot(grad, head_of(k), part.at[k])
         if k == 2:
             hidden_send(*sends, 0, 0).start()
             hidden_send(*sends, 1, 0).start()
-        elif k:
+        else:
             hidden_send(*sends, k // 2, 1).start()
 
 
@@ -101,25 +103,71 @@
         hidden_send(part, early_in, final_in, send_sem, recv_sem, side, 2).start()
 
 
-def hidden_sum(part, early_in, final_in, send_sem, recv_sem, out):
-    step = 64
-    sends = (part, early_in, final_in, send_sem, recv_sem)
+def hidden_finish(*sends):
     for stage in (1, 2):
         for side in range(2):
             hidden_send(*sends, side, stage).wait_recv()
-
-    @pl.loop(0, out.shape[0] // step)
-    def _(i):
-        rows = pl.ds(pl.multiple_of(i * step, step), step)
-        out[rows] = (
-            part[0, rows].astype(jnp.float32)
-            + final_in[0, rows].astype(jnp.float32)
-            + final_in[1, rows].astype(jnp.float32)
-        ).astype(jnp.bfloat16)
-
     for stage in range(3):
         for side in range(2):
             hidden_send(*sends, side, stage).wait_send()
+
+
+def finish_kernel(
+    near_a, landed_a, near_b, landed_b, near_p, landed_p, weight, query_out, passage_out, weight_out
+):
+    def total(near, landed):
+        result = near[...].astype(jnp.float32) + landed[0].astype(jnp.float32)
+        return (result + landed[1].astype(jnp.float32)).astype(jnp.bfloat16)
+
+    early = pl.program_id(0) < 2
+
+    @pl.when(early)
+    def _():
+        query_out[...] = total(near_a, landed_a)
+
+    @pl.when(jnp.logical_not(early))
+    def _():
+        query_out[...] = total(near_b, landed_b)
+
+    passage_out[...] = total(near_p, landed_p)
+    weight_out[...] = weight[...]
+
+
+def finish(near_a, landed_a, near_b, landed_b, near_p, landed_p, weight):
+    rows, width = near_p.shape
+    block = rows // 4
+    share = weight.shape[0] // 4
+    first = lambda i: jnp.minimum(i, 1)
+    second = lambda i: jnp.maximum(i - 2, 0)
+    same = lambda i: i
+
+    def near(index):
+        return pl.BlockSpec((block, width), lambda i: (index(i), 0))
+
+    def landed(index):
+        return pl.BlockSpec((2, block, width), lambda i: (0, index(i), 0))
+
+    weight_spec = pl.BlockSpec((share, width), lambda i: (i, 0))
+    return pl.pallas_call(
+        finish_kernel,
+        grid=(4,),
+        out_shape=(
+            jax.ShapeDtypeStruct((rows, width), jnp.bfloat16),
+            jax.ShapeDtypeStruct((rows, width), jnp.bfloat16),
+            jax.ShapeDtypeStruct(weight.shape, jnp.float32),
+        ),
+        in_specs=[
+            near(first),
+            landed(first),
+            near(second),
+            landed(second),
+            near(same),
+            landed(same),
+            weight_spec,
+        ],
+        out_specs=(near(same), near(same), weight_spec),
+        name="finish",
+    )(near_a, landed_a, near_b, landed_b, near_p, landed_p, weight)
 
 
 def place():
@@ -222,18 +270,28 @@
 
 
 def tail_kernel(
-    d_query,
     block_sums,
-    own_terms,
-    passage_norm,
     inverses,
+    d_query_hbm,
+    own_hbm,
+    norm_hbm,
     query_hbm,
     passage_hbm,
     head_hbm,
     weight_out,
-    hidden_out,
+    near_out,
+    final_in,
+    query_near_out,
+    query_final_in,
+    query_part,
+    query_early_in,
+    query_depth_send,
+    query_depth_recv,
+    d_query,
+    passage_norm,
     home,
     d_total,
+    extra_sem,
     d_passage,
     inner,
     inner_in,
@@ -252,7 +310,6 @@
     second_in,
     part,
     early_in,
-    final_in,
     load_sem,
     hidden_load_sem,
     depth_send,
@@ -272,21 +329,24 @@
     def chunk_of(i):
         return lax.rem(y + 1 + lax.div(i, 2), 4) * 2 + lax.rem(lax.div(x, 2) + 1 + i, 2)
 
-    def hidden_loads(i, slot):
+    def hidden_load(side, i, slot):
         columns = pl.ds(pl.multiple_of(chunk_of(i) * wide, wide), wide)
-        return (
-            pltpu.make_async_copy(
-                query_hbm.at[:, columns], query.at[slot], hidden_load_sem.at[0, slot]
-            ),
-            pltpu.make_async_copy(
-                passage_hbm.at[:, columns], passage.at[slot], hidden_load_sem.at[1, slot]
-            ),
+        source, buffer = ((query_hbm, query), (passage_hbm, passage))[side]
+        return pltpu.make_async_copy(
+            source.at[:, columns], buffer.at[slot], hidden_load_sem.at[side, slot]
         )
 
     for k in DEPTH_ORDER:
         head_load(head_hbm, head, load_sem, k).start()
-    for copy in hidden_loads(0, 0) + hidden_loads(1, 1):
+    extra_loads = (
+        pltpu.make_async_copy(d_query_hbm, d_query, extra_sem.at[0]),
+        pltpu.make_async_copy(own_hbm, d_total, extra_sem.at[1]),
+        pltpu.make_async_copy(norm_hbm, passage_norm, extra_sem.at[2]),
+    )
+    for copy in extra_loads:
         copy.start()
+    for i in range(2):
+        hidden_load(0, i, i).start()
     greet(
         [{"dp": plane_peer(offset)} for offset in OFFSETS]
         + [depth_partner(k) for k in (1, 2, 3)]
@@ -307,10 +367,38 @@
         home_copy(j).start()
     home[:, share_rows(dp), share_cols(dp)] = block_sums[pl.ds(dp * 4, 4)]
     inner[4:8] = jnp.zeros((4, 128), jnp.float32)
+    for copy in extra_loads:
+        copy.wait()
+    for k in DEPTH_ORDER:
+        head_load(head_hbm, head, load_sem, k).wait()
+    query_args = (query_part, query_early_in, query_final_in, query_depth_send, query_depth_recv)
+    second_half = d_query.at[query_near_out.shape[0] :]
+    hidden_parts(second_half, lambda k: head.at[k], *query_args)
+    hidden_dot(second_half, head.at[0], query_near_out)
+
+    @pl.loop(0, 8)
+    def _(i):
+        slot = lax.rem(i, 2)
+        hidden_load(0, i, slot).wait()
+        chunk = chunk_of(i)
+        for j in range(2):
+            columns = slice(j * 2 * rows, (j + 1) * 2 * rows)
+            total = lax.dot_general(
+                query[slot, :, columns], d_query[...], ROW_CONTRACT, preferred_element_type=jnp.float32
+            )
+            summed[chunk * 2 + j] = total.astype(jnp.bfloat16).reshape(2, rows, 2 * half)
+
+        @pl.when(i < 6)
+        def _():
+            hidden_load(0, i + 2, slot).start()
+
+    for i in range(2):
+        hidden_load(1, i, i).start()
+    hidden_merge(*query_args)
     for j in range(31):
         home_copy(j).wait_recv()
     for b in range(4):
-        total = own_terms[b] + home[b].astype(jnp.float32)
+        total = d_total[b] + home[b].astype(jnp.float32)
         d_total[b] = total
         inner[b : b + 1] = as_row(
             jnp.sum(passage_norm[b].astype(jnp.float32) * total, axis=1, keepdims=True)
@@ -322,8 +410,6 @@
         d_passage[b * 128 : (b + 1) * 128] = embed_grad(
             inverses[0, b : b + 1], passage_norm[b], d_total[b], total_inner[b : b + 1]
         )
-    for k in DEPTH_ORDER:
-        head_load(head_hbm, head, load_sem, k).wait()
     depth_args = (part, early_in, final_in, depth_send, depth_recv)
     hidden_parts(d_passage, lambda k: head.at[k], *depth_args)
 
@@ -362,26 +448,23 @@
 
     def produce(i):
         slot = lax.rem(i, 2)
-        for copy in hidden_loads(i, slot):
-            copy.wait()
+        hidden_load(1, i, slot).wait()
         chunk = chunk_of(i)
         for j in range(2):
             columns = slice(j * 2 * rows, (j + 1) * 2 * rows)
+            chip = chunk * 2 + j
             total = lax.dot_general(
-                query[slot, :, columns], d_query[...], ROW_CONTRACT, preferred_element_type=jnp.float32
-            ) + lax.dot_general(
                 passage[slot, :, columns],
                 d_passage[...],
                 ROW_CONTRACT,
                 preferred_element_type=jnp.float32,
-            )
-            summed[chunk * 2 + j] = total.astype(jnp.bfloat16).reshape(2, rows, 2 * half)
+            ) + summed[chip].reshape(2 * rows, 2 * half).astype(jnp.float32)
+            summed[chip] = total.astype(jnp.bfloat16).reshape(2, rows, 2 * half)
             core_copy(chunk * 2 + j).start()
 
         @pl.when(i < 6)
         def _():
-            for copy in hidden_loads(i + 2, slot):
-                copy.start()
+            hidden_load(1, i + 2, slot).start()
 
     def combine(i):
         for j in range(2):
@@ -399,9 +482,9 @@
                 def _():
                     copy.start()
 
-    @pl.loop(0, 9)
+    @pl.loop(0, 10)
     def _(i):
-        @pl.when(i == 4)
+        @pl.when(i == 7)
         def _():
             hidden_merge(*depth_args)
 
@@ -409,9 +492,11 @@
         def _():
             produce(i)
 
-        @pl.when(i > 0)
+        @pl.when(i > 1)
         def _():
-            combine(i - 1)
+            combine(i - 2)
+
+    hidden_dot(d_passage, head.at[0], near_out)
 
     def first_arrival(side, k, other):
         return remote(
@@ -456,7 +541,8 @@
             weight_out[:, side * half : (side + 1) * half] += second_in[side, k - 1].astype(
                 jnp.float32
             )
-    hidden_sum(*depth_args, hidden_out)
+    hidden_finish(*query_args)
+    hidden_finish(*depth_args)
     for j in range(31):
         home_copy(j).wait_send()
     depth_finish(*inner_args)
@@ -498,12 +584,22 @@
         out_shape=(
             jax.ShapeDtypeStruct((share, width), jnp.float32),
             jax.ShapeDtypeStruct((rows, width), bf16),
+            jax.ShapeDtypeStruct((2, rows, width), bf16),
+            jax.ShapeDtypeStruct((rows // 2, width), bf16),
+            jax.ShapeDtypeStruct((2, rows // 2, width), bf16),
         ),
-        in_specs=[vmem] * 5 + [hbm] * 3,
-        out_specs=(vmem, vmem),
+        in_specs=[vmem] * 2 + [hbm] * 6,
+        out_specs=(vmem,) + (vmem, pl.BlockSpec(memory_space=pltpu.HBM)) * 2,
         scratch_shapes=[
+            pltpu.VMEM((4, rows // 2, width), bf16),
+            pltpu.VMEM((2, rows // 4, width), bf16),
+            dma((2, 3)),
+            dma((2, 3)),
+            pltpu.VMEM((rows, width), bf16),
+            pltpu.VMEM((4, 128, width), bf16),
             pltpu.VMEM((4, 128, width), bf16),
             pltpu.VMEM((4, 128, width), jnp.float32),
+            dma((3,)),
             pltpu.VMEM((rows, width), bf16),
             pltpu.VMEM((8, 128), jnp.float32),
             pltpu.VMEM((3, 8, 128), jnp.float32),
@@ -522,7 +618,6 @@
             pltpu.VMEM((2, 3, share, width // 2), bf16),
             pltpu.VMEM((4, rows, width), bf16),
             pltpu.VMEM((2, rows // 2, width), bf16),
-            pltpu.VMEM((2, rows, width), bf16),
             dma((4,)),
             dma((2, 2)),
             dma((2, 3)),
@@ -539,11 +634,11 @@
         ),
         name="tail",
     )(
+        block_sums,
+        inverses,
         d_query,
-        block_sums,
         own_terms,
         passage_norm,
-        inverses,
         query_hidden,
         passage_hidden,
         head_weight,
@@ -563,7 +658,8 @@
     d_query_embed,
     own_terms,
     returned,
-    hidden_out,
+    near_out,
+    final_in,
     head,
     hidden,
     embed,
@@ -582,7 +678,6 @@
     outgoing,
     part,
     early_in,
-    final_in,
     squares,
     squares_in,
     load_sem,
@@ -648,7 +743,8 @@
         want_copy(j).start()
     all_wanted[dp] = wanted[...]
     for b in range(4):
-        targets[b] = jnp.broadcast_to(as_column(positions[b : b + 1]), (128, 128))
+        row = positions[b * 128 : (b + 1) * 128].astype(jnp.float32).reshape(1, 128)
+        targets[b] = jnp.broadcast_to(as_column(row), (128, 128))
 
     def project(side):
         @pl.loop(0, 4)
@@ -861,7 +957,9 @@
             inner[b : b + 1],
         )
     depth_args = (part, early_in, final_in, depth_send, depth_recv)
-    hidden_parts(d_query_embed, lambda k: head.at[lax.rem(mp + k, 4)], *depth_args)
+    first_half = d_query_embed.at[: near_out.shape[0]]
+    hidden_parts(first_half, lambda k: head.at[lax.rem(mp + k, 4)], *depth_args)
+    hidden_dot(first_half, head.at[mp], near_out)
     for k in (1, 3, 2):
         loss_copy(k).wait_recv()
     for b in range(4):
@@ -885,7 +983,7 @@
             return_copy(j, b).wait_send()
             return_copy(j, b).wait_recv()
 
-    hidden_sum(*depth_args, hidden_out)
+    hidden_finish(*depth_args)
 
 
 def main_part(query_hidden, passage_hidden, head_weight, neg_blocks, pos_ids):
@@ -893,7 +991,6 @@
     f32 = jnp.float32
     rows = query_hidden.shape[0]
     width = head_weight.shape[1]
-    positions = pos_ids.reshape(4, 128).astype(f32)
     vmem = pl.BlockSpec(memory_space=pltpu.VMEM)
     smem = pl.BlockSpec(memory_space=pltpu.SMEM)
     hbm = pl.BlockSpec(memory_space=pl.ANY)
@@ -908,10 +1005,12 @@
             jax.ShapeDtypeStruct((rows, width), bf16),
             jax.ShapeDtypeStruct((4, 128, width), f32),
             jax.ShapeDtypeStruct((32, 16, 16, 256), bf16),
-            jax.ShapeDtypeStruct((rows, width), bf16),
+            jax.ShapeDtypeStruct((rows // 2, width), bf16),
+            jax.ShapeDtypeStruct((2, rows // 2, width), bf16),
         ),
         in_specs=[hbm, hbm, hbm, smem, vmem],
-        out_specs=(vmem, vmem, vmem, smem, vmem, vmem, vmem, vmem),
+        out_specs=(vmem, vmem, vmem, smem, vmem, vmem, vmem, vmem)
+        + (pl.BlockSpec(memory_space=pltpu.HBM),),
         scratch_shapes=[
             pltpu.VMEM((4, width, width), bf16),
             pltpu.VMEM((2, 4, rows, width), bf16),
@@ -929,9 +1028,8 @@
             pltpu.VMEM((4, 128, 640), bf16),
             pltpu.VMEM((4, 128, 128), f32),
             pltpu.VMEM((16, 128, width), bf16),
-            pltpu.VMEM((4, rows, width), bf16),
-            pltpu.VMEM((2, rows // 2, width), bf16),
-            pltpu.VMEM((2, rows, width), bf16),
+            pltpu.VMEM((4, rows // 2, width), bf16),
+            pltpu.VMEM((2, rows // 4, width), bf16),
             pltpu.VMEM((3, 8, 128), f32),
             pltpu.VMEM((3, 3, 8, 128), f32),
             dma((3, 4)),
@@ -959,7 +1057,7 @@
             collective_id=1, has_side_effects=True, vmem_limit_bytes=VMEM_LIMIT
         ),
         name="main_part",
-    )(query_hidden, passage_hidden, head_weight, neg_blocks, positions)
+    )(query_hidden, passage_hidden, head_weight, neg_blocks, pos_ids)
 
 
 def local(query_hidden, passage_hidden, head_weight, neg_blocks, pos_ids):
@@ -971,10 +1069,11 @@
         d_query,
         own_terms,
         returned,
-        query_grad,
+        near_a,
+        landed_a,
     ) = main_part(query_hidden, passage_hidden, head_weight, neg_blocks, pos_ids)
     block_sums = add_returned(table, returned.reshape(512, 16, 256))
-    grad_weight, passage_grad = tail(
+    weight, near_p, landed_p, near_b, landed_b = tail(
         d_query,
         block_sums,
         own_terms,
@@ -984,6 +1083,9 @@
         passage_hidden,
         head_weight,
     )
+    query_grad, passage_grad, grad_weight = finish(
+        near_a, landed_a, near_b, landed_b, near_p, landed_p, weight
+    )
     return losses.reshape(512), grad_weight, query_grad, passage_grad
 
 

time: 231 us -> 221 us (0.957)
  local copies, waits for them, and re-layouts: 5.7 us -> 0.58 us
  Pallas kernels: 224 us -> 219 us
    pallas_call x1, Pallas kernels: 144 us -> 135 us  [main_part(): pl.pallas_call(main_kernel, out_shape=(jax.ShapeDtypeStruct((4, 128), f32...]
    unnamed x8 -> x3, local copies, waits for them, and re-layouts: 5.7 us -> 0.58 us
    pallas_call x0 -> x1, Pallas kernels: none -> 5.03 us  [finish(): pl.pallas_call(finish_kernel, grid=(4,), out_shape=(jax.ShapeDtypeStruct(...]
where the time goes in v6:
time: 221 us; the launch traced here: 220 us
  Pallas kernels  219 us (99%)
    pallas_call x1, Pallas kernels, main_part(): pl.pallas_call(main_kernel, out_shape=(jax.ShapeDtypeStruct((4, 128), f32...  135 us
    pallas_call x1, Pallas kernels, tail(): pl.pallas_call(tail_kernel, out_shape=(jax.ShapeDtypeStruct((share, width...  73.2 us
    pallas_call x1, Pallas kernels, add_returned(): pl.pallas_call(add_kernel, out_shape=jax.ShapeDtypeStruct((128, 16, 256),...  5.49 us
    pallas_call x1, Pallas kernels, finish(): pl.pallas_call(finish_kernel, grid=(4,), out_shape=(jax.ShapeDtypeStruct(...  5.03 us

profile of v6, /device:TPU:1, one launch (start us, length us, event | category | flops | bytes accessed | tf_op | source)
XLA Modules:
  0.0 220.4 jit_solution(6727944079036330030)
XLA Ops:
  0.6 135.5 %main_part.1 = (f32[4,128]{1,0:T(4,128)}, bf16[4,128,1024]{2,1,0:T(8,128)(2,1)}, f32[2,8,128]{2,1,0:T(8,128)}, s32[512]{0:T(512)}, bf16[512,1024]{1,0:T(8,128)(2...) custom-call(bf16[512,4096]{1,0:T(8,128)(2,1)} %query_hbm.3, ...), custom_call_target="tpu_custom_call" | custom-call | tf_op jit(solution)/shard_map/main_part/pallas_call | solution.py:998
  136.1 5.5 %add_returned.1.block_sums = bf16[128,16,256]{2,1,0:T(8,128)(2,1)} custom-call(s32[512]{0:T(512)} %get-tuple-element.24.table, bf16[512,16,256]{2,1,0:T(8,128)(2,1)} %bitcast.2), custom_call_target="tpu_custom_call" | custom-call | tf_op jit(solution)/shard_map/add_returned/pallas_call | solution.py:262
  141.6 73.2 %tail.1 = (f32[128,1024]{1,0:T(8,128)}, bf16[512,1024]{1,0:T(8,128)(2,1)}, bf16[2,512,1024]{2,1,0:T(8,128)(2,1)}, bf16[256,1024]{1,0:T(8,128)(2,1)}, bf16[2,256,1024]{2,1,0:T(8,128)(2,1)}) custom-call(bf16[128,16,256]{2,1,0:T(8,128)(2,1)} %add_returned.1.block_sums, f32[2,8,128]{2,1,0:T(8,128)} %get-tuple-element.26.inverses, ...), custom_call_target="tpu_custom_call" | custom-call | tf_op jit(solution)/shard_map/tail/pallas_call | solution.py:582
  214.8 0.0 copy-start
  214.8 5.0 %finish.1 = (bf16[512,1024]{1,0:T(8,128)(2,1)}, bf16[512,1024]{1,0:T(8,128)(2,1)}, f32[128,1024]{1,0:T(8,128)}) custom-call(bf16[256,1024]{1,0:T(8,128)(2,1)} %get-tuple-element.22.near_a, bf16[2,256,1024]{2,1,0:T(8,128)(2,1)} %get-tuple-element.23.landed_a, bf16[256,1024]{1,0:T(8,128)(2,1)} %get-tuple-element.30.near_b, ...), custom_call_target="tpu_custom_call" | custom-call | tf_op jit(solution)/shard_map/finish/pallas_call | solution.py:151
  219.8 0.0 copy-done
  219.8 0.6 copy.10
Async XLA Ops:
  214.8 5.0 %copy-start = (f32[4,128]{1,0:T(4,128)S(1)}, f32[4,128]{1,0:T(4,128)}, u32[]{:S(2)}) copy-start(f32[4,128]{1,0:T(4,128)} %get-tuple-element.21) | copy-start | bytes 6148
